TPU v7x, 512 devices: a whole 4x8x8 slice. The times are simulated.
512 devices in a mesh: img: 32 (over x, y), blk: 16 (over z, core).
Axes of the slice: x: 4, y: 8, z: 8, core: 2. Of those that a mesh axis runs over, the one named last changes fastest.
Arguments:
- images: bfloat16 [128, 28, 1792], P('img'), may hold values from -6 to 6
- filters: bfloat16 [8192, 576], P('blk'), may hold values from -0.5 to 0.5
- phases: float32 [8192], P('blk'), may hold values from -3.140625 to 3.140625
- labels: int32 [25088], P('img'), may hold values from 0 to 149
- weights: float32 [150, 8192], P(None, 'blk'), may hold values from -6 to 6
Outputs:
- new_weights: float32 [150, 8192], P(None, 'blk')
- residual: float32 [150, 25088], P(None, 'img')
All inputs are finite; a program needn't handle non-finite values.
Results may differ from a plain program's by a relative error of at most 0.015.
Values may be sent and summed in bfloat16 or wider, within the bound.
No kernel may reach another device: no remote copies, remote signals or barrier semaphores. Data moves between devices by JAX's collectives and lax.ppermute only.
A program may use at most 64 MiB of HBM per device.

v0:
```python
import math

import jax
import jax.numpy as jnp
from jax import lax
from jax.sharding import PartitionSpec as P

SIDE = 28
CHAN = 64
FILT = 512
LABELS = 150
ITERS = 2


RIDGE = 0.5
DAMPING = 0.75


def total_of_pieces(shard, axis):
    return lax.all_gather(shard, axis).astype(jnp.float32).sum(0)


def padded_to(lines, devices):
    spare = -len(lines) % devices
    return jnp.pad(lines, [(0, spare)] + [(0, 0)] * (lines.ndim - 1))


def joined_along(blocks, dim):
    shape = list(blocks.shape[1:])
    shape[dim] *= blocks.shape[0]
    return jnp.moveaxis(blocks, 0, dim).reshape(shape)


def copy_for_each(shard, axis):
    devices = lax.axis_size(axis)
    return lax.all_to_all(
        jnp.broadcast_to(shard[None], (devices, *shard.shape)), axis, 0, 0, tiled=True
    )


def collect(shard, axis, dim):
    return joined_along(copy_for_each(shard, axis), dim)


def split_up(shard, dim, devices):
    before, after = (shard.shape[:dim], shard.shape[dim + 1 :])
    return jnp.moveaxis(shard.reshape(*before, devices, -1, *after), dim, 0)


def sum_at_owner(shard, axis, dim):
    blocks = split_up(shard, dim, lax.axis_size(axis))
    arrived = lax.all_to_all(blocks, axis, split_axis=0, concat_axis=0, tiled=True)
    return arrived.sum(axis=0)


def sum_by_parts(shard, axes):
    lines = shard.reshape(-1)
    padded = padded_to(lines, lax.axis_size(axes))
    whole = collect(sum_at_owner(padded, axes, 0), axes, 0)
    return lax.slice_in_dim(whole, 0, len(lines)).reshape(shard.shape)


def block_features(images, filter_rows, phase_rows):
    count_images = images.shape[0]
    pictures = images.reshape(count_images, SIDE, SIDE, CHAN)
    kernel = filter_rows.reshape(filter_rows.shape[0], 3, 3, CHAN)
    response = lax.conv_general_dilated(
        pictures,
        kernel,
        (2, 2),
        ((1, 1), (1, 1)),
        dimension_numbers=("NHWC", "OHWI", "CNHW"),
        preferred_element_type=jnp.float32,
    )
    response = response.reshape(filter_rows.shape[0], count_images * (SIDE // 2) ** 2)
    return (math.sqrt(2.0) * jnp.cos(response + phase_rows[:, None])).astype(jnp.bfloat16)


def solve_with(factor, projected):
    middle = lax.linalg.triangular_solve(
        factor, projected, left_side=False, lower=True, transpose_a=True
    )
    return lax.linalg.triangular_solve(
        factor, middle, left_side=False, lower=True, transpose_a=False
    )


def predict(weight_now, features, shrink):
    partial_value = shrink * jnp.dot(
        weight_now.astype(jnp.bfloat16), features, preferred_element_type=jnp.float32
    )
    return total_of_pieces(partial_value.astype(jnp.bfloat16), "blk").astype(jnp.float32)


def shards(images, filters, phases, labels, weights):
    features = block_features(images, filters, phases)
    image_groups = lax.axis_size("img")
    pixels = labels.shape[0] * image_groups
    features_all = FILT * lax.axis_size("blk")
    shrink = 1.0 / math.sqrt(features_all)
    expand = math.sqrt(features_all)
    targets = (labels[None, :] == jnp.arange(LABELS, dtype=jnp.int32)[:, None]).astype(jnp.float32)
    identity = jnp.eye(FILT, dtype=jnp.float32)
    local_gram = lax.dot_general(
        features, features, (((1,), (1,)), ((), ())), preferred_element_type=jnp.float32
    )
    predicted = predict(weights, features, shrink)
    gram = sum_by_parts(local_gram, "img") + RIDGE * pixels * identity
    factor = jnp.linalg.cholesky(gram)
    residual = targets - predicted
    weight_now = weights
    for step in range(ITERS):
        local_projection = lax.dot_general(
            residual.astype(jnp.bfloat16),
            features,
            (((1,), (1,)), ((), ())),
            preferred_element_type=jnp.float32,
        )
        projected = sum_by_parts(local_projection, "img")
        weight_now = weight_now + DAMPING * (expand * solve_with(factor, projected))
        residual = targets - predict(weight_now, features, shrink)
    return (weight_now, residual)


def solution(mesh):
    return jax.shard_map(
        shards,
        mesh=mesh,
        in_specs=(P("img", None, None), P("blk", None), P("blk"), P("img"), P(None, "blk")),
        out_specs=(P(None, "blk"), P(None, "img")),
        check_vma=False,
    )
```

profile of v0, /device:TPU:1, one launch (start us, length us, event | category | flops | bytes accessed | tf_op | source)
XLA Modules:
  0.0 456.8 jit_solution(13946562588334397632)
XLA Ops:
  7.2 1.9 reshape.116
  9.1 14.1 %multiply_convert_fusion.1 = (bf16[512,4,14,14]{0,1,3,2:T(4,128)(2,1)}, f32[512,4,14,14]{0,1,3,2:T(4,128)S(1)}) fusion(f32[512]{0:T(512)} %param.11, bf16[512,3,3,64]{0,3,2,1:T(8,128)(2,1)S(1)} %bitcast.122, bf16[4,28,28,64]{3,2,0,1:T(8,128)(2,1)S(1)} %reshape.116), kind=kOutput, calls=%fused_computation.6 | convolution fusion | flops 441868288 | bytes 3401728 | tf_op jit(solution)/shard_map/conv_general_dilated | solution.py:67
  23.8 1.4 reshape.118
  25.1 6.4 %multiply_convert_fusion = bf16[512,784]{0,1:T(8,128)(2,1)S(1)} fusion(f32[512,784]{0,1:T(8,128)} %reshape.118, f32[512]{0:T(512)S(1)} %copy-done.6), kind=kLoop, calls=%fused_computation.5 | loop fusion | flops 1204224 | bytes 2410496 | tf_op jit(solution)/shard_map/convert_element_type | solution.py:76
  31.6 1.2 fusion.5
  32.8 0.8 convolution_bitcast_fusion
  33.5 1.2 all_to_all.39
  34.8 34.9 %all_to_all.48 = f32[32,1,8192]{2,1,0:T(1,128)S(1)} all-to-all(f32[32,1,8192]{2,1,0:T(1,128)S(1)} %all_to_all.39), channel_id=1, replica_groups=mesh['img'=32,'blk'=16] {'img'}, dimensions={0} | all-to-all | bytes 2097152 | tf_op jit(solution)/shard_map/all_to_all | solution.py:52
  69.7 0.7 reduce_sum.54
  70.4 1.9 broadcast_in_dim.7
  72.4 8.7 %all-to-all-start.1 = ((f32[32,1,8192]{2,1,0:T(1,128)}), f32[32,1,8192]{2,1,0:T(1,128)S(1)}, u32[]{:S(2)}, u32[]{:S(2)}) async-start(f32[32,1,8192]{2,1,0:T(1,128)} %broadcast_in_dim.7), calls=%async_computation.1 | async-start | bytes 2097152 | tf_op jit(solution)/shard_map/all_to_all | solution.py:36
  81.1 25.0 %all-to-all-done.1 = f32[32,1,8192]{2,1,0:T(1,128)S(1)} async-done(((f32[32,1,8192]{2,1,0:T(1,128)}), f32[32,1,8192]{2,1,0:T(1,128)S(1)}, u32[]{:S(2)}, u32[]{:S(2)}) %all-to-all-start.1) | async-done | bytes 1048608 | tf_op jit(solution)/shard_map/all_to_all | solution.py:36
  106.1 2.6 reduce.30
  108.7 1.2 reshape_reshape.9
  109.8 1.6 copy.63
  111.4 1.1 select_add_fusion
  112.5 1.6 copy.64
  114.3 1.0 copy-done.3
  115.2 11.7 %cholesky.103 = f32[128,128]{1,0:T(8,128)S(1)} custom-call(f32[128,128]{1,0:T(8,128)S(1)} %cholesky.263), custom_call_target="Cholesky" | custom-call | tf_op jit(solution)/shard_map/jit(cholesky)/cholesky | solution.py:109
  127.1 9.8 %custom-call.33 = f32[1,128,128]{1,2,0:T(8,128)S(1)} custom-call(f32[1,128,128]{2,1,0:T(8,128)S(1)} %get-tuple-element.115), custom_call_target="InvertDiagBlocksLowerTriangular" | custom-call | tf_op jit(solution)/shard_map/jit(cholesky)/cholesky | solution.py:109
  136.9 1.2 fusion.42
  138.3 1.3 convolution_subtract_fusion
  139.5 11.9 %cholesky.215 = f32[128,128]{1,0:T(8,128)S(1)} custom-call(f32[128,128]{1,0:T(8,128)S(1)} %cholesky.267), custom_call_target="Cholesky" | custom-call | tf_op jit(solution)/shard_map/jit(cholesky)/cholesky | solution.py:109
  151.6 9.8 %custom-call.34 = f32[1,128,128]{1,2,0:T(8,128)S(1)} custom-call(f32[1,128,128]{2,1,0:T(8,128)S(1)} %get-tuple-element.113), custom_call_target="InvertDiagBlocksLowerTriangular" | custom-call | tf_op jit(solution)/shard_map/jit(cholesky)/cholesky | solution.py:109
  161.9 1.5 convolution_subtract_fusion.1
  163.4 11.7 %cholesky.236 = f32[128,128]{1,0:T(8,128)S(1)} custom-call(f32[128,128]{1,0:T(8,128)S(1)} %cholesky.272), custom_call_target="Cholesky" | custom-call | tf_op jit(solution)/shard_map/jit(cholesky)/cholesky | solution.py:109
  175.3 9.8 %custom-call.35 = f32[1,128,128]{1,2,0:T(8,128)S(1)} custom-call(f32[1,128,128]{2,1,0:T(8,128)S(1)} %get-tuple-element.111), custom_call_target="InvertDiagBlocksLowerTriangular" | custom-call | tf_op jit(solution)/shard_map/jit(cholesky)/cholesky | solution.py:109
  185.4 1.3 convolution_subtract_fusion.14
  186.7 12.1 %cholesky.253 = f32[128,128]{1,0:T(8,128)S(1)} custom-call(f32[128,128]{1,0:T(8,128)S(1)} %convolution_subtract_fusion.14), custom_call_target="Cholesky" | custom-call | tf_op jit(solution)/shard_map/jit(cholesky)/cholesky | solution.py:109
  198.9 0.7 compare_reduce_fusion.2
  202.1 3.0 convert_reduce_fusion.2
  205.4 1.2 all_to_all.40
  206.7 8.1 %all-to-all-start.2 = ((f32[32,1,2400]{2,1,0:T(1,128)}), f32[32,1,2400]{2,1,0:T(1,128)}, u32[]{:S(2)}, u32[]{:S(2)}) async-start(f32[32,1,2400]{2,1,0:T(1,128)} %all_to_all.40), calls=%async_computation.2 | async-start | bytes 622592 | tf_op jit(solution)/shard_map/all_to_all | solution.py:52
  214.9 0.7 compare_reduce_fusion
  216.4 8.3 %all-to-all-done.2 = f32[32,1,2400]{2,1,0:T(1,128)} async-done(((f32[32,1,2400]{2,1,0:T(1,128)}), f32[32,1,2400]{2,1,0:T(1,128)}, u32[]{:S(2)}, u32[]{:S(2)}) %all-to-all-start.2) | async-done | bytes 307232 | tf_op jit(solution)/shard_map/all_to_all | solution.py:52
  224.8 1.2 reduce_sum.56
  225.9 0.9 broadcast_in_dim.9
  226.8 6.7 %all-to-all-start.3 = ((f32[32,1,2400]{2,1,0:T(1,128)}), f32[32,1,2400]{2,1,0:T(1,128)S(1)}, u32[]{:S(2)}, u32[]{:S(2)}) async-start(f32[32,1,2400]{2,1,0:T(1,128)} %broadcast_in_dim.9), calls=%async_computation.3 | async-start | bytes 622592 | tf_op jit(solution)/shard_map/all_to_all | solution.py:36
  233.6 11.2 %while.8 = (s32[]{:T(128)}, f32[512,512]{0,1:T(8,128)S(1)}, s32[4,2]{0,1:T(2,128)S(1)}, f32[4,128,128]{2,1,0:T(8,128)}, s32[]{:T(128)}) while((s32[]{:T(128)}, f32[512,512]{0,1:T(8,128)S(1)}, s32[4,2]{0,1:T(2,128)S(1)}, f32[4,128,128]{2,1,0:T(8,128)}, s32[]{:T(128)}) %tuple.57), condition=%wide.while_cond, body=%wide.while_body.sunk | while | flops 2 | bytes 393329 | solution.py:80
  234.4 1.3 dynamic-slice.14
  237.2 1.3 dynamic-slice.14
  239.9 1.3 dynamic-slice.14
  242.7 1.3 dynamic-slice.14
  244.8 40.1 %custom-call.38 = f32[4,128,128]{1,2,0:T(8,128)S(1)} custom-call(f32[4,128,128]{2,1,0:T(8,128)} %get-tuple-element.32), custom_call_target="InvertDiagBlocksLowerTriangular" | custom-call | tf_op jit(solution)/shard_map/triangular_solve/custom-call.3 | solution.py:80
  284.9 1.5 reduce.31
  286.4 1.3 reshape_reshape.10
  292.1 1.2 fusion.4
  293.3 51.8 %all-gather.12.cloned.1.call-done = bf16[16,150,784]{2,1,0:T(8,128)(2,1)} async-done(((bf16[1,150,784]{2,1,0:T(8,128)(2,1)}), bf16[16,150,784]{2,1,0:T(8,128)(2,1)}) %all-gather.12.cloned.1.call-update) | async-done | bytes 3763216 | tf_op jit(solution)/shard_map/all_gather | solution.py:20
  345.2 3.0 convert_reduce_fusion.1
  348.1 1.1 fusion.14
  349.2 2.2 all_to_all.41
  351.4 19.8 %all_to_all.49 = f32[32,1,2400]{2,1,0:T(1,128)} all-to-all(f32[32,1,2400]{2,1,0:T(1,128)} %all_to_all.41), channel_id=1, replica_groups=mesh['img'=32,'blk'=16] {'img'}, dimensions={0} | all-to-all | bytes 614400 | tf_op jit(solution)/shard_map/all_to_all | solution.py:52
  371.2 1.2 reduce_sum.58
  372.5 17.3 %all_to_all.50 = f32[32,1,2400]{2,1,0:T(1,128)} all-to-all(f32[32,1,2400]{2,1,0:T(1,128)S(1)} %broadcast_in_dim.10), channel_id=1, replica_groups=mesh['img'=32,'blk'=16] {'img'}, dimensions={0} | all-to-all | bytes 614400 | tf_op jit(solution)/shard_map/all_to_all | solution.py:36
  389.8 2.4 reduce.32
  392.2 2.0 reshape_reshape.11
  394.2 1.2 fusion.69
  395.4 1.2 convolution_subtract_fusion.5
  396.8 1.2 convolution_subtract_fusion.4
  398.3 1.3 convolution_subtract_fusion.11
  402.2 1.2 fusion.3
  403.4 42.8 %all-gather.14.cloned.1.call-done = bf16[16,150,784]{2,1,0:T(8,128)(2,1)} async-done(((bf16[1,150,784]{2,1,0:T(8,128)(2,1)}), bf16[16,150,784]{2,1,0:T(8,128)(2,1)}) %all-gather.14.cloned.1.call-update) | async-done | bytes 3763216 | tf_op jit(solution)/shard_map/all_gather | solution.py:20
  446.2 3.0 convert_reduce_fusion
  449.2 0.9 convert_subtract_fusion
  (92 shorter events, 16.7 us)
Async XLA Ops:
  7.2 2.0 copy-start
  7.2 194.9 %all-gather.10.cloned.1.call-start = ((), (), s32[]{:S(2)}) async-start(), calls=%async_computation.6 | async-start | bytes 4630528 | tf_op jit(solution)/shard_map/all_gather | solution.py:20
  23.8 1.4 copy-start.6
  25.1 6.4 %copy-start.1 = (f32[150,512]{1,0:T(8,128)S(1)}, f32[150,512]{1,0:T(8,128)}, u32[]{:S(2)}) copy-start(f32[150,512]{1,0:T(8,128)} %param.13) | copy-start | bytes 921604
  25.1 7.6 %copy-start.7 = (bf16[512,4,14,14]{0,1,3,2:T(4,128)(2,1)S(1)}, bf16[512,4,14,14]{0,1,3,2:T(4,128)(2,1)}, u32[]{:S(2)}) copy-start(bf16[512,4,14,14]{0,1,3,2:T(4,128)(2,1)} %get-tuple-element.116) | copy-start | bytes 2408452
  72.4 33.7 %all-to-all-start.1 = ((f32[32,1,8192]{2,1,0:T(1,128)}), f32[32,1,8192]{2,1,0:T(1,128)S(1)}, u32[]{:S(2)}, u32[]{:S(2)}) async-start(f32[32,1,8192]{2,1,0:T(1,128)} %broadcast_in_dim.7), calls=%async_computation.1 | async-start | bytes 2097152 | tf_op jit(solution)/shard_map/all_to_all | solution.py:36
  114.2 1.0 copy-start.3
  202.1 3.0 copy-start.5
  206.7 18.1 %all-to-all-start.2 = ((f32[32,1,2400]{2,1,0:T(1,128)}), f32[32,1,2400]{2,1,0:T(1,128)}, u32[]{:S(2)}, u32[]{:S(2)}) async-start(f32[32,1,2400]{2,1,0:T(1,128)} %all_to_all.40), calls=%async_computation.2 | async-start | bytes 622592 | tf_op jit(solution)/shard_map/all_to_all | solution.py:52
  226.8 58.1 %all-to-all-start.3 = ((f32[32,1,2400]{2,1,0:T(1,128)}), f32[32,1,2400]{2,1,0:T(1,128)S(1)}, u32[]{:S(2)}, u32[]{:S(2)}) async-start(f32[32,1,2400]{2,1,0:T(1,128)} %broadcast_in_dim.9), calls=%async_computation.3 | async-start | bytes 622592 | tf_op jit(solution)/shard_map/all_to_all | solution.py:36
  233.5 111.7 %all-gather.12.cloned.1.call-start = ((), (), s32[]{:S(2)}) async-start(), calls=%async_computation.7 | async-start | bytes 4630528 | tf_op jit(solution)/shard_map/all_gather | solution.py:20
  288.8 3.2 copy-start.2
  293.3 152.9 %all-gather.14.cloned.1.call-start = ((), (), s32[]{:S(2)}) async-start(), calls=%async_computation.8 | async-start | bytes 4630528 | tf_op jit(solution)/shard_map/all_gather | solution.py:20
  402.2 47.0 %copy-start.4 = (f32[150,512]{1,0:T(8,128)}, f32[150,512]{1,0:T(8,128)S(1)}, u32[]{:S(2)}) copy-start(f32[150,512]{1,0:T(8,128)S(1)} %fusion.13) | copy-start | bytes 921604
Sparse Core Ops, SparseCore 0:
  32.9 51.1 all-gather.9
  293.4 51.7 all-gather.11
  403.6 42.5 all-gather.13
where the time goes:
time: 465 us; the launch traced here: 457 us
  other arithmetic  146 us (31%)
  waiting for transfers between devices  128 us (28%)
  blocking collectives  72 us (15%)
  matrix products  37.8 us (8%)
  local copies, waits for them, and re-layouts  31.6 us (7%)
  starting transfers between devices  23.7 us (5%)
  between operations  17.1 us (4%)
    all_gather x3, waiting for transfers between devices, total_of_pieces(): return lax.all_gather(shard, axis).astype(jnp.float32).sum(0)  94.6 us
    another operation x14, other arithmetic, shards(): factor = jnp.linalg.cholesky(gram)  79.1 us
    all_to_all x2, blocking collectives, sum_at_owner(): lax.all_to_all(blocks, axis, split_axis=0, concat_axis=0, tiled=True)  54.7 us
    another operation x4, other arithmetic, solve_with(): lax.linalg.triangular_solve(factor, projected, left_side=False, lower=Tru...  40.3 us
    all_to_all x2, waiting for transfers between devices, copy_for_each(): lax.all_to_all(jnp.broadcast_to(shard[None], (devices, *shard.shape)), ax...  25 us
    all_to_all x1, blocking collectives, copy_for_each(): lax.all_to_all(jnp.broadcast_to(shard[None], (devices, *shard.shape)), ax...  17.3 us
    all_to_all x2, starting transfers between devices, copy_for_each(): lax.all_to_all(jnp.broadcast_to(shard[None], (devices, *shard.shape)), ax...  15.4 us
    conv_general_dilated x1, matrix products, block_features(): lax.conv_general_dilated(pictures, kernel, (2, 2), ((1, 1), (1, 1)), dime...  14.1 us
  transfers between devices with their start and end apart: 6, of which 4 were waited for; matrix products, arithmetic and copies ran while one was open for 32% of the time, Pallas kernels for 0%

commit v1 on v0

v1 whole, which is shorter than its diff:
```python
import math

import jax
import jax.numpy as jnp
import numpy as np
from jax import lax
from jax.experimental import pallas as pl
from jax.experimental.pallas import tpu as pltpu
from jax.sharding import PartitionSpec as P

SIDE = 28
CHAN = 64
FILT = 512
LABELS = 150
ITERS = 2
RIDGE = 0.5
DAMPING = 0.75

OUT = SIDE // 2
PAIR = 2 * CHAN
DEEP = 6 * PAIR
ROWS = 160
TILE = 128
BF16 = jnp.bfloat16
F32 = jnp.float32


def cosine_coefficients(degree):
    nodes = np.cos((np.arange(200) + 0.5) * math.pi / 200)
    squares = (nodes + 1) * 0.5 * math.pi**2
    fit = np.polynomial.Chebyshev.fit(
        squares, math.sqrt(2.0) * np.cos(np.sqrt(squares)), degree, domain=[0, math.pi**2]
    )
    return [float(c) for c in fit.convert(kind=np.polynomial.Polynomial).coef]


COS = cosine_coefficients(7)


def scaled_cosine(x):
    turns = jnp.floor(x * (0.5 / math.pi) + 0.5)
    y = (x - turns * 6.28125) - turns * (2 * math.pi - 6.28125)
    u = y * y
    value = u * COS[-1] + COS[-2]
    for c in COS[-3::-1]:
        value = value * u + c
    return value


def up8(n):
    return -(-n // 8) * 8


def call(kernel, outs, *args, scratch=(), name=None, flops=0):
    specs = [
        pl.BlockSpec(memory_space=pltpu.SMEM if a.dtype == jnp.int32 and a.ndim == 1 else pltpu.VMEM)
        for a in args
    ]
    size = sum(math.prod(a.shape) * a.dtype.itemsize for a in (*args, *outs))
    return pl.pallas_call(
        kernel,
        out_shape=outs,
        in_specs=specs,
        out_specs=[pl.BlockSpec(memory_space=pltpu.VMEM)] * len(outs),
        scratch_shapes=scratch,
        name=name,
        cost_estimate=pl.CostEstimate(flops=flops, bytes_accessed=size, transcendentals=0),
    )(*args)


def contract_last(a, b):
    return lax.dot_general(a, b, (((1,), (1,)), ((), ())), preferred_element_type=F32)


def store_prediction(stack_ref, weights, features, shrink):
    for t in range(features.shape[1] // TILE):
        part = jnp.dot(weights, features[:, t * TILE : (t + 1) * TILE], preferred_element_type=F32)
        stack_ref[t * ROWS : (t + 1) * ROWS] = (part * shrink).astype(BF16)
    used = features.shape[1] // TILE * ROWS
    if used < stack_ref.shape[0]:
        stack_ref[used:] = jnp.zeros((stack_ref.shape[0] - used, TILE), BF16)


def feature_kernel(img, filt, phase, feat, gram, rows32, patches, taps):
    sides, count = img.shape[:2]
    per = OUT * OUT
    patches[...] = jnp.zeros_like(patches)
    for c in range(OUT):
        for row in range(sides):
            rows32[row * count : (row + 1) * count] = img[row, :, c * PAIR : (c + 1) * PAIR].astype(F32)
        for n in range(count):
            even = rows32[pl.ds(n, OUT, stride=2 * count), :]
            odd = rows32[pl.ds(count + n, OUT, stride=2 * count), :]
            for side in range(2):
                at = c + 1 - side
                if at >= OUT:
                    continue
                first = n * per + at
                patches[2 + side, pl.ds(first, OUT, stride=OUT), :] = even
                patches[4 + side, pl.ds(first, OUT, stride=OUT), :] = odd
                patches[side, pl.ds(first + OUT, OUT - 1, stride=OUT), :] = odd[: OUT - 1]
    windows = jnp.concatenate([patches[k].astype(BF16) for k in range(DEEP // PAIR)], axis=1)
    third = DEEP // 3
    for k in range(3):
        taps[k * third : k * third + CHAN] = jnp.zeros((CHAN, FILT), BF16)
        taps[k * third + CHAN : (k + 1) * third] = filt[k * 3 * CHAN : (k + 1) * 3 * CHAN]
    for block in range(FILT // TILE):
        rows = slice(block * TILE, (block + 1) * TILE)
        response = lax.dot_general(
            taps[:, rows], windows, (((0,), (1,)), ((), ())), preferred_element_type=F32
        )
        turned = jnp.broadcast_to(phase[:, rows], (TILE, TILE)).T
        values = scaled_cosine(response + turned[:, :1])
        live = lax.broadcasted_iota(jnp.int32, values.shape, 1) < count * per
        feat[rows] = jnp.where(live, values, 0.0).astype(BF16)
    at = 0
    for i in range(FILT // TILE):
        for j in range(i + 1):
            gram[at : at + TILE] = contract_last(
                feat[i * TILE : (i + 1) * TILE], feat[j * TILE : (j + 1) * TILE]
            )
            at += TILE


def first_predict_kernel(shrink, weights, feat, stack, wide):
    wide[...] = jnp.zeros_like(wide)
    wide[:LABELS] = weights[...]
    store_prediction(stack, wide[...].astype(BF16), feat[...], shrink)


def summed(ref, parts):
    rows = ref.shape[0] // parts
    total = ref[:rows].astype(F32)
    for k in range(1, parts):
        total += ref[k * rows : (k + 1) * rows].astype(F32)
    return total


def copies(ref, value, parts):
    rows = value.shape[0]
    for k in range(parts):
        ref[k * rows : (k + 1) * rows] = value


def residual_kernel(parts, place, got, labels, out):
    total = summed(got, parts)
    rows = total.shape[0]
    line = lax.broadcasted_iota(jnp.int32, total.shape, 0) + place[0] * rows
    targets = jnp.zeros_like(total)
    for t in range(labels.shape[0]):
        targets += jnp.where(line - t * ROWS == labels[t : t + 1], 1.0, 0.0)
    copies(out, (targets - total).astype(BF16), parts)


def gram_kernel(parts, got, out):
    copies(out, summed(got, parts), parts)


def unstacked(ref, tiles):
    return jnp.concatenate([ref[t * ROWS : (t + 1) * ROWS] for t in range(tiles)], axis=1)


def project_kernel(parts, got, feat, out, spread):
    tiles = feat.shape[1] // TILE
    projected = contract_last(unstacked(got, tiles), feat[...])
    own = ROWS // parts
    rows = spread.shape[0] // parts
    lanes = FILT // TILE
    if own * lanes < rows:
        spread[...] = jnp.zeros_like(spread)
    for k in range(own):
        for t in range(lanes):
            spread[pl.ds(k * lanes + t, parts, stride=rows), :] = projected[
                k * parts : (k + 1) * parts, t * TILE : (t + 1) * TILE
            ]
    out[...] = spread[...].astype(out.dtype)


def two_halves(x):
    high = x.astype(BF16)
    return high, (x - high.astype(F32)).astype(BF16)


def inverse_kernel(ridge, got, matrix, inverse, left, value):
    at = 0
    for i in range(FILT // TILE):
        for j in range(i + 1):
            part = got[at : at + TILE]
            at += TILE
            if i == j:
                eye = lax.broadcasted_iota(jnp.int32, part.shape, 0) == lax.broadcasted_iota(jnp.int32, part.shape, 1)
                part = part + jnp.where(eye, ridge, 0.0)
            else:
                value[j * TILE : (j + 1) * TILE, i * TILE : (i + 1) * TILE] = part.T
            value[i * TILE : (i + 1) * TILE, j * TILE : (j + 1) * TILE] = part
    h = value[...]
    high, rest = two_halves(h)
    matrix[:FILT] = high
    matrix[FILT:] = rest
    left[:, :FILT] = high
    left[:, FILT : 2 * FILT] = high
    left[:, 2 * FILT :] = rest
    largest = jnp.max(jnp.sum(jnp.abs(h), axis=0, keepdims=True))
    scale = 1.0 / largest
    low = 0.98 * ridge * scale
    eye = lax.broadcasted_iota(jnp.int32, h.shape, 0) == lax.broadcasted_iota(jnp.int32, h.shape, 1)
    gain = 4.0 / ((1.0 + low) * (1.0 + low))
    value[...] = gain * scale * (jnp.where(eye, 1.0 + low, 0.0) - scale * h)

    def more(low):
        return low < 1.0 - 1e-4

    def step(low):
        gain = 4.0 / ((1.0 + low) * (1.0 + low))
        x = value[...]
        xh, xl = two_halves(x)
        y = jnp.dot(left[...], jnp.concatenate([xh, xl, xh], axis=0), preferred_element_type=F32)
        yh, yl = two_halves(y)
        xy = jnp.dot(
            jnp.concatenate([xh, xh, xl], axis=1),
            jnp.concatenate([yh, yl, yh], axis=0),
            preferred_element_type=F32,
        )
        value[...] = gain * ((1.0 + low) * x - xy)
        return jnp.minimum(gain * low, 1.0)

    lax.while_loop(more, step, gain * low)
    high, rest = two_halves(value[...])
    inverse[:FILT] = high
    inverse[FILT:] = rest


def times(x, halves):
    rows = x.shape[0]
    both = jnp.concatenate([x.astype(BF16).astype(F32), x - x.astype(BF16).astype(F32)], axis=0).astype(BF16)
    found = jnp.dot(both, halves[:FILT], preferred_element_type=F32) + jnp.dot(
        both, halves[FILT:], preferred_element_type=F32
    )
    return found[:rows] + found[rows:]


def solve_kernel(parts, factor, place, got, weights, matrix, inverse, own_out, out, folded, wide):
    own = ROWS // parts
    lanes = FILT // TILE
    rows = got.shape[0] // parts
    tall = folded.shape[0] // lanes
    folded[...] = jnp.zeros_like(folded)
    folded[:rows] = summed(got, parts)
    projected = jnp.concatenate([folded[pl.ds(t, tall, stride=lanes), :] for t in range(lanes)], axis=1)
    change = times(projected, inverse)
    for _ in range(2):
        change += times(projected - times(change, matrix), inverse)
    if weights.shape[0] == tall:
        now = weights[...]
    else:
        wide[...] = jnp.zeros_like(wide)
        wide[:LABELS] = weights[...]
        held = [wide[pl.ds(place[0] + k * parts, 1), :] for k in range(own)]
        if own < tall:
            held.append(jnp.zeros((tall - own, FILT), F32))
        now = jnp.concatenate(held, axis=0)
    new = now + factor * change
    own_out[...] = new
    for t in range(lanes):
        folded[pl.ds(t, tall, stride=lanes), :] = new[:, t * TILE : (t + 1) * TILE]
    copies(out, folded[:rows].astype(out.dtype), parts)


def predict_kernel(parts, shrink, keep, got, feat, *refs):
    stack = refs[0]
    spread = refs[-1]
    own = ROWS // parts
    rows = got.shape[0] // parts
    lanes = FILT // TILE
    spread[...] = got[...].astype(F32)
    weights = jnp.concatenate(
        [
            jnp.concatenate(
                [spread[pl.ds(k * lanes + t, parts, stride=rows), :] for t in range(lanes)], axis=1
            )
            for k in range(own)
        ],
        axis=0,
    )
    if keep:
        refs[1][...] = weights[:LABELS]
    store_prediction(stack, weights.astype(BF16), feat[...], shrink)


def output_kernel(got, out):
    tiles = -(-out.shape[1] // TILE)
    for t in range(tiles):
        wide = min(TILE, out.shape[1] - t * TILE)
        out[:, t * TILE : t * TILE + wide] = got[t * ROWS : t * ROWS + LABELS, :wide].astype(F32)


def exchange(x, axis):
    parts = lax.axis_size(axis)
    pieces = x.reshape(parts, x.shape[0] // parts, x.shape[1])
    return lax.all_to_all(pieces, axis, 0, 0, tiled=True).reshape(x.shape)


def shards(images, filters, phases, labels, weights):
    groups, blocks = lax.axis_size("img"), lax.axis_size("blk")
    here = labels.shape[0]
    ridge = RIDGE * here * groups
    shrink = 1.0 / math.sqrt(FILT * blocks)
    factor = DAMPING * math.sqrt(FILT * blocks)
    lane_tiles = -(-here // TILE)
    padded = lane_tiles * TILE
    stack_rows = up8(-(-lane_tiles * ROWS // blocks)) * blocks
    fold_rows = up8(ROWS // groups * (FILT // TILE)) * groups
    gram_rows = (FILT // TILE) * (FILT // TILE + 1) // 2 * TILE
    tall = up8(ROWS // groups)

    img_place = lax.axis_index("img").astype(jnp.int32).reshape(1)
    blk_place = lax.axis_index("blk").astype(jnp.int32).reshape(1)
    label_tiles = jnp.pad(labels, (0, padded - here), constant_values=-100000).reshape(lane_tiles, TILE)

    def shape(*dims, dtype=F32):
        return jax.ShapeDtypeStruct(dims, dtype)

    feat, gram_part = call(
        feature_kernel, [shape(FILT, padded, dtype=BF16), shape(gram_rows, TILE)],
        images.transpose(1, 0, 2), filters.T, phases.reshape(1, FILT),
        scratch=[
            pltpu.VMEM((SIDE * images.shape[0], PAIR), F32),
            pltpu.VMEM((DEEP // PAIR, padded, PAIR), F32),
            pltpu.VMEM((DEEP, FILT), BF16),
        ],
        name="features", flops=2 * 10**9,
    )
    (stack,) = call(
        lambda *r: first_predict_kernel(shrink, *r), [shape(stack_rows, TILE, dtype=BF16)], weights, feat,
        scratch=[pltpu.VMEM((ROWS, FILT), F32)], name="predict", flops=10**8,
    )

    def residual_of(stack):
        (mine,) = call(
            lambda *r: residual_kernel(blocks, *r), [shape(stack_rows, TILE, dtype=BF16)],
            blk_place, exchange(stack, "blk"), label_tiles, name="residual",
        )
        return exchange(mine, "blk")

    def projection_of(residual):
        (parts,) = call(
            lambda *r: project_kernel(groups, *r), [shape(fold_rows, TILE)],
            residual, feat, scratch=[pltpu.VMEM((fold_rows, TILE), F32)], name="project", flops=10**8,
        )
        return exchange(parts, "img")

    residual = residual_of(stack)
    (gram_sum,) = call(
        lambda *r: gram_kernel(groups, *r), [shape(gram_rows, TILE)], exchange(gram_part, "img"), name="gram",
    )
    matrix, inverse = call(
        lambda *r: inverse_kernel(ridge, *r), [shape(2 * FILT, FILT, dtype=BF16)] * 2,
        exchange(gram_sum, "img"),
        scratch=[pltpu.VMEM((FILT, 3 * FILT), BF16), pltpu.VMEM((FILT, FILT), F32)],
        name="inverse", flops=14 * 10**9,
    )
    own = weights
    for step in range(ITERS):
        last = step == ITERS - 1
        kind = F32 if last else BF16
        projected = projection_of(residual)
        own, spread = call(
            lambda *r: solve_kernel(groups, factor, *r), [shape(tall, FILT), shape(fold_rows, TILE, dtype=kind)],
            img_place, projected, own, matrix, inverse,
            scratch=[pltpu.VMEM((tall * (FILT // TILE), TILE), F32), pltpu.VMEM((ROWS, FILT), F32)],
            name="solve", flops=10**8,
        )
        found = call(
            lambda *r: predict_kernel(groups, shrink, last, *r),
            [shape(stack_rows, TILE, dtype=BF16)] + ([shape(LABELS, FILT)] if last else []),
            exchange(spread, "img"), feat,
            scratch=[pltpu.VMEM((fold_rows, TILE), F32)], name="predict", flops=10**8,
        )
        residual = residual_of(found[0])
    (out,) = call(output_kernel, [shape(LABELS, here)], residual, name="output")
    return (found[1], out)


def solution(mesh):
    return jax.shard_map(
        shards,
        mesh=mesh,
        in_specs=(P("img", None, None), P("blk", None), P("blk"), P("img"), P(None, "blk")),
        out_specs=(P(None, "blk"), P(None, "img")),
        check_vma=False,
    )
```

time: 465 us -> 275 us (0.59); the launches traced: 457 us -> 273 us
  other arithmetic: 146 us -> 0 us
  waiting for transfers between devices: 128 us -> 43.6 us
  blocking collectives: 72 us -> 150 us
  Pallas kernels: 0 us -> 50.4 us
  matrix products: 37.8 us -> 0 us
  local copies, waits for them, and re-layouts: 31.6 us -> 2.74 us
  between operations: 17.1 us -> 0.7 us
    another operation x18 -> x0, other arithmetic: 119 us -> none  [the longest x14 79.1 us: shards(): factor = jnp.linalg.cholesky(gram)]
    all_gather x3 -> x0, waiting for transfers between devices: 94.6 us -> none  [total_of_pieces(): return lax.all_gather(shard, axis).astype(jnp.float32).sum(0)]
    all_to_all x3 -> x8, blocking collectives: 72 us -> 150 us  [exchange(): return lax.all_to_all(pieces, axis, 0, 0, tiled=True).reshape(x.shape)]
    pallas_call x0 -> x14, Pallas kernels: none -> 50.4 us  [call(): pl.pallas_call(kernel, out_shape=outs, in_specs=specs, out_specs=[pl.Bloc...]
    another operation x34 -> x0, matrix products: 18 us -> none  [the longest x14 7.72 us: solve_with(): lax.linalg.triangular_solve(factor, projected, left_side=False, lower=Tru...]
    another operation x38 -> x0, local copies, waits for them, and re-layouts: 17.6 us -> none  [the longest x21 11 us: solve_with(): lax.linalg.triangular_solve(factor, projected, left_side=False, lower=Tru...]
    conv_general_dilated x1 -> x0, matrix products: 14.1 us -> none  [block_features(): lax.conv_general_dilated(pictures, kernel, (2, 2), ((1, 1), (1, 1)), dime...]
    reduce_sum x6 -> x0, other arithmetic: 12 us -> none  [the longest x3 8.94 us: total_of_pieces(): return lax.all_gather(shard, axis).astype(jnp.float32).sum(0)]
  transfers between devices with their start and end apart: 6 -> 4, of which waited for: 4 -> 3; matrix products, arithmetic and copies ran while one was open for 32% -> 0% of each run, Pallas kernels for 0% -> 8%
where the time goes in v1:
time: 275 us; the launch traced here: 273 us
  blocking collectives  150 us (55%)
  Pallas kernels  50.4 us (18%)
  waiting for transfers between devices  43.6 us (16%)
  starting transfers between devices  25.9 us (9%)
    all_to_all x8, blocking collectives, exchange(): return lax.all_to_all(pieces, axis, 0, 0, tiled=True).reshape(x.shape)  150 us
    pallas_call x14, Pallas kernels, call(): pl.pallas_call(kernel, out_shape=outs, in_specs=specs, out_specs=[pl.Bloc...  50.4 us
    all_to_all x4, waiting for transfers between devices, exchange(): return lax.all_to_all(pieces, axis, 0, 0, tiled=True).reshape(x.shape)  43.6 us
    all_to_all x4, starting transfers between devices, exchange(): return lax.all_to_all(pieces, axis, 0, 0, tiled=True).reshape(x.shape)  25.9 us
  transfers between devices with their start and end apart: 4, of which 3 were waited for; matrix products, arithmetic and copies ran while one was open for 0% of the time, Pallas kernels for 8%

profile of v1, /device:TPU:1, one launch (start us, length us, event | category | flops | bytes accessed | tf_op | source)
XLA Modules:
  0.0 273.1 jit_solution(10061191237750947823)
XLA Ops:
  0.6 5.4 %features.1 = (bf16[512,896]{1,0:T(8,128)(2,1)}, f32[1280,128]{1,0:T(8,128)}) custom-call(bf16[28,4,1792]{2,1,0:T(4,128)(2,1)} %bitcast.55, bf16[576,512]{1,0:T(8,128)(2,1)} %bitcast.54, f32[1,512]{1,0:T(1,128)} %bitcast.56), custom_call_target="tpu_custom_call" | custom-call | flops 2000000000 | bytes 2566144 | tf_op jit(solution)/shard_map/features/pallas_call | solution.py:60
  6.0 2.4 predict.3
  8.4 24.2 %all_to_all.60 = bf16[16,72,128]{2,1,0:T(8,128)(2,1)} all-to-all(bf16[16,72,128]{2,1,0:T(8,128)(2,1)} %bitcast.48), channel_id=1, replica_groups=mesh['img'=32,'blk'=16] {'blk'}, dimensions={0} | all-to-all | bytes 589824 | tf_op jit(solution)/shard_map/all_to_all | solution.py:300
  32.6 9.7 %all-to-all-start.3 = ((f32[32,40,128]{2,1,0:T(8,128)}), f32[32,40,128]{2,1,0:T(8,128)S(1)}, u32[]{:S(2)}, u32[]{:S(2)}) async-start(f32[32,40,128]{2,1,0:T(8,128)} %bitcast.12), calls=%async_computation.3 | async-start | bytes 1310720 | tf_op jit(solution)/shard_map/all_to_all | solution.py:300
  42.3 0.0 copy-start.4
  42.3 0.7 copy-done.4
  43.0 0.6 pad_bitcast_fusion.r_2_
  43.6 1.8 residual.3
  45.4 16.0 %all-to-all-done.3 = f32[32,40,128]{2,1,0:T(8,128)S(1)} async-done(((f32[32,40,128]{2,1,0:T(8,128)}), f32[32,40,128]{2,1,0:T(8,128)S(1)}, u32[]{:S(2)}, u32[]{:S(2)}) %all-to-all-start.3) | async-done | bytes 655392 | tf_op jit(solution)/shard_map/all_to_all | solution.py:300
  61.4 0.0 copy-start
  61.4 4.7 %all-to-all-start.1 = ((bf16[16,72,128]{2,1,0:T(8,128)(2,1)}), bf16[16,72,128]{2,1,0:T(8,128)(2,1)S(1)}, u32[]{:S(2)}, u32[]{:S(2)}) async-start(bf16[16,72,128]{2,1,0:T(8,128)(2,1)} %bitcast.40), calls=%async_computation.1 | async-start | bytes 589824 | tf_op jit(solution)/shard_map/all_to_all | solution.py:300
  66.1 0.0 copy-done
  66.1 2.0 gram.1
  68.1 10.6 %all-to-all-done.1 = bf16[16,72,128]{2,1,0:T(8,128)(2,1)S(1)} async-done(((bf16[16,72,128]{2,1,0:T(8,128)(2,1)}), bf16[16,72,128]{2,1,0:T(8,128)(2,1)S(1)}, u32[]{:S(2)}, u32[]{:S(2)}) %all-to-all-start.1) | async-done | bytes 294944 | tf_op jit(solution)/shard_map/all_to_all | solution.py:300
  78.7 0.0 copy-start.2
  78.7 0.7 copy-done.2
  79.4 5.5 %all-to-all-start.4 = ((f32[32,40,128]{2,1,0:T(8,128)}), f32[32,40,128]{2,1,0:T(8,128)S(1)}, u32[]{:S(2)}, u32[]{:S(2)}) async-start(f32[32,40,128]{2,1,0:T(8,128)} %bitcast.32), calls=%async_computation.4 | async-start | bytes 1310720 | tf_op jit(solution)/shard_map/all_to_all | solution.py:300
  84.9 2.5 project.2
  87.4 17.0 %all-to-all-done.4 = f32[32,40,128]{2,1,0:T(8,128)S(1)} async-done(((f32[32,40,128]{2,1,0:T(8,128)}), f32[32,40,128]{2,1,0:T(8,128)S(1)}, u32[]{:S(2)}, u32[]{:S(2)}) %all-to-all-start.4) | async-done | bytes 655392 | tf_op jit(solution)/shard_map/all_to_all | solution.py:300
  104.4 0.0 copy-start.3
  104.4 6.1 %all-to-all-start.2 = ((f32[32,24,128]{2,1,0:T(8,128)}), f32[32,24,128]{2,1,0:T(8,128)S(1)}, u32[]{:S(2)}, u32[]{:S(2)}) async-start(f32[32,24,128]{2,1,0:T(8,128)} %bitcast.34), calls=%async_computation.2 | async-start | bytes 786432 | tf_op jit(solution)/shard_map/all_to_all | solution.py:300
  110.5 0.0 copy-done.3
  110.5 16.2 %inverse.1 = (bf16[1024,512]{1,0:T(8,128)(2,1)}, bf16[1024,512]{1,0:T(8,128)(2,1)}) custom-call(f32[1280,128]{1,0:T(8,128)} %bitcast.50), custom_call_target="tpu_custom_call" | custom-call | flops 14000000000 | bytes 2752512 | tf_op jit(solution)/shard_map/inverse/pallas_call | solution.py:60
  126.7 0.0 all-to-all-done.2
  126.7 0.0 copy-start.1
  126.7 0.7 copy-done.1
  127.4 3.6 %solve.2 = (f32[8,512]{1,0:T(8,128)}, bf16[768,128]{1,0:T(8,128)(2,1)}) custom-call(s32[1]{0:T(128)} %bitcast.r_0_, f32[768,128]{1,0:T(8,128)} %bitcast.33, f32[150,512]{1,0:T(8,128)} %r_2_.1, bf16[1024,512]{1,0:T(8,128)(2,1)} %get-tuple-element.13.r_3_, bf16[1024,512]{1,0:T(8,128)(2,1)} %get-tuple-element.14.r_4_), custom_call_target="tpu_custom_call" | custom-call | flops 100000000 | bytes 3010564 | tf_op jit(solution)/shard_map/solve/pallas_call | solution.py:60
  131.1 18.7 %all_to_all.61 = bf16[32,24,128]{2,1,0:T(8,128)(2,1)} all-to-all(bf16[32,24,128]{2,1,0:T(8,128)(2,1)} %bitcast.53), channel_id=1, replica_groups=mesh['img'=32,'blk'=16] {'img'}, dimensions={0} | all-to-all | bytes 393216 | tf_op jit(solution)/shard_map/all_to_all | solution.py:300
  149.8 2.5 predict.4
  152.3 19.4 %all_to_all.62 = bf16[16,72,128]{2,1,0:T(8,128)(2,1)} all-to-all(bf16[16,72,128]{2,1,0:T(8,128)(2,1)} %bitcast.46), channel_id=1, replica_groups=mesh['img'=32,'blk'=16] {'blk'}, dimensions={0} | all-to-all | bytes 589824 | tf_op jit(solution)/shard_map/all_to_all | solution.py:300
  171.7 1.8 residual.4
  173.5 15.6 %all_to_all.63 = bf16[16,72,128]{2,1,0:T(8,128)(2,1)} all-to-all(bf16[16,72,128]{2,1,0:T(8,128)(2,1)} %bitcast.44), channel_id=1, replica_groups=mesh['img'=32,'blk'=16] {'blk'}, dimensions={0} | all-to-all | bytes 589824 | tf_op jit(solution)/shard_map/all_to_all | solution.py:300
  189.0 2.5 project.3
  191.5 19.0 %all_to_all.64 = f32[32,24,128]{2,1,0:T(8,128)} all-to-all(f32[32,24,128]{2,1,0:T(8,128)} %bitcast.36), channel_id=1, replica_groups=mesh['img'=32,'blk'=16] {'img'}, dimensions={0} | all-to-all | bytes 786432 | tf_op jit(solution)/shard_map/all_to_all | solution.py:300
  210.5 3.6 %solve.3 = (f32[8,512]{1,0:T(8,128)}, f32[768,128]{1,0:T(8,128)}) custom-call(s32[1]{0:T(128)} %bitcast.r_0_, f32[768,128]{1,0:T(8,128)} %bitcast.37, f32[8,512]{1,0:T(8,128)} %get-tuple-element.16.r_2_, bf16[1024,512]{1,0:T(8,128)(2,1)} %get-tuple-element.13.r_3_, bf16[1024,512]{1,0:T(8,128)(2,1)} %get-tuple-element.14.r_4_), custom_call_target="tpu_custom_call" | custom-call | flops 100000000 | bytes 2916356 | tf_op jit(solution)/shard_map/solve/pallas_call | solution.py:60
  214.2 17.4 %all_to_all.65 = f32[32,24,128]{2,1,0:T(8,128)} all-to-all(f32[32,24,128]{2,1,0:T(8,128)} %bitcast.51), channel_id=1, replica_groups=mesh['img'=32,'blk'=16] {'img'}, dimensions={0} | all-to-all | bytes 786432 | tf_op jit(solution)/shard_map/all_to_all | solution.py:300
  231.5 2.5 predict.5
  234.0 20.0 %all_to_all.66 = bf16[16,72,128]{2,1,0:T(8,128)(2,1)} all-to-all(bf16[16,72,128]{2,1,0:T(8,128)(2,1)} %bitcast.52), channel_id=1, replica_groups=mesh['img'=32,'blk'=16] {'blk'}, dimensions={0} | all-to-all | bytes 589824 | tf_op jit(solution)/shard_map/all_to_all | solution.py:300
  254.0 1.8 residual.5
  255.8 15.6 %all_to_all.67 = bf16[16,72,128]{2,1,0:T(8,128)(2,1)} all-to-all(bf16[16,72,128]{2,1,0:T(8,128)(2,1)} %bitcast.42), channel_id=1, replica_groups=mesh['img'=32,'blk'=16] {'blk'}, dimensions={0} | all-to-all | bytes 589824 | tf_op jit(solution)/shard_map/all_to_all | solution.py:300
  271.3 1.8 output.1
Async XLA Ops:
  32.6 28.7 %all-to-all-start.3 = ((f32[32,40,128]{2,1,0:T(8,128)}), f32[32,40,128]{2,1,0:T(8,128)S(1)}, u32[]{:S(2)}, u32[]{:S(2)}) async-start(f32[32,40,128]{2,1,0:T(8,128)} %bitcast.12), calls=%async_computation.3 | async-start | bytes 1310720 | tf_op jit(solution)/shard_map/all_to_all | solution.py:300
  42.3 0.7 copy-start.4
  61.4 4.7 %copy-start = (f32[32,40,128]{2,1,0:T(8,128)}, f32[32,40,128]{2,1,0:T(8,128)S(1)}, u32[]{:S(2)}) copy-start(f32[32,40,128]{2,1,0:T(8,128)S(1)} %all-to-all-done.3) | copy-start | bytes 1966084
  61.4 17.3 %all-to-all-start.1 = ((bf16[16,72,128]{2,1,0:T(8,128)(2,1)}), bf16[16,72,128]{2,1,0:T(8,128)(2,1)S(1)}, u32[]{:S(2)}, u32[]{:S(2)}) async-start(bf16[16,72,128]{2,1,0:T(8,128)(2,1)} %bitcast.40), calls=%async_computation.1 | async-start | bytes 589824 | tf_op jit(solution)/shard_map/all_to_all | solution.py:300
  78.7 0.7 copy-start.2
  79.4 25.0 %all-to-all-start.4 = ((f32[32,40,128]{2,1,0:T(8,128)}), f32[32,40,128]{2,1,0:T(8,128)S(1)}, u32[]{:S(2)}, u32[]{:S(2)}) async-start(f32[32,40,128]{2,1,0:T(8,128)} %bitcast.32), calls=%async_computation.4 | async-start | bytes 1310720 | tf_op jit(solution)/shard_map/all_to_all | solution.py:300
  104.4 6.1 %copy-start.3 = (f32[32,40,128]{2,1,0:T(8,128)}, f32[32,40,128]{2,1,0:T(8,128)S(1)}, u32[]{:S(2)}) copy-start(f32[32,40,128]{2,1,0:T(8,128)S(1)} %all-to-all-done.4) | copy-start | bytes 1966084
  104.4 22.3 %all-to-all-start.2 = ((f32[32,24,128]{2,1,0:T(8,128)}), f32[32,24,128]{2,1,0:T(8,128)S(1)}, u32[]{:S(2)}, u32[]{:S(2)}) async-start(f32[32,24,128]{2,1,0:T(8,128)} %bitcast.34), calls=%async_computation.2 | async-start | bytes 786432 | tf_op jit(solution)/shard_map/all_to_all | solution.py:300
  126.7 0.7 copy-start.1

commit v2 on v1

--- a/solution.py
+++ b/solution.py
@@ -63,6 +63,7 @@
         in_specs=specs,
         out_specs=[pl.BlockSpec(memory_space=pltpu.VMEM)] * len(outs),
         scratch_shapes=scratch,
+        compiler_params=pltpu.CompilerParams(vmem_limit_bytes=20 * 2**20),
         name=name,
         cost_estimate=pl.CostEstimate(flops=flops, bytes_accessed=size, transcendentals=0),
     )(*args)
@@ -149,7 +150,7 @@
     targets = jnp.zeros_like(total)
     for t in range(labels.shape[0]):
         targets += jnp.where(line - t * ROWS == labels[t : t + 1], 1.0, 0.0)
-    copies(out, (targets - total).astype(BF16), parts)
+    out[...] = (targets - total).astype(BF16)
 
 
 def gram_kernel(parts, got, out):
@@ -337,10 +338,10 @@
 
     def residual_of(stack):
         (mine,) = call(
-            lambda *r: residual_kernel(blocks, *r), [shape(stack_rows, TILE, dtype=BF16)],
+            lambda *r: residual_kernel(blocks, *r), [shape(stack_rows // blocks, TILE, dtype=BF16)],
             blk_place, exchange(stack, "blk"), label_tiles, name="residual",
         )
-        return exchange(mine, "blk")
+        return lax.all_gather(mine, "blk", tiled=True)
 
     def projection_of(residual):
         (parts,) = call(
@@ -362,10 +363,9 @@
     own = weights
     for step in range(ITERS):
         last = step == ITERS - 1
-        kind = F32 if last else BF16
         projected = projection_of(residual)
         own, spread = call(
-            lambda *r: solve_kernel(groups, factor, *r), [shape(tall, FILT), shape(fold_rows, TILE, dtype=kind)],
+            lambda *r: solve_kernel(groups, factor, *r), [shape(tall, FILT), shape(fold_rows, TILE, dtype=BF16)],
             img_place, projected, own, matrix, inverse,
             scratch=[pltpu.VMEM((tall * (FILT // TILE), TILE), F32), pltpu.VMEM((ROWS, FILT), F32)],
             name="solve", flops=10**8,

time: 275 us -> 238 us (0.87)
  Pallas kernels: 50.4 us -> 27.3 us
  waiting for transfers between devices: 43.6 us -> 29 us
  blocking collectives: 150 us -> 137 us
  starting transfers between devices: 25.9 us -> 37.3 us
    all_to_all x8 -> x5, blocking collectives: 150 us -> 91.3 us  [exchange(): return lax.all_to_all(pieces, axis, 0, 0, tiled=True).reshape(x.shape)]
    all_gather x0 -> x3, blocking collectives: none -> 45.8 us  [residual_of(): return lax.all_gather(mine, 'blk', tiled=True)]
    pallas_call x14, Pallas kernels: 50.4 us -> 27.3 us  [call(): pl.pallas_call(kernel, out_shape=outs, in_specs=specs, out_specs=[pl.Bloc...]
    all_to_all x4, waiting for transfers between devices: 43.6 us -> 29 us  [exchange(): return lax.all_to_all(pieces, axis, 0, 0, tiled=True).reshape(x.shape)]
    all_to_all x4, starting transfers between devices: 25.9 us -> 37.3 us  [exchange(): return lax.all_to_all(pieces, axis, 0, 0, tiled=True).reshape(x.shape)]
    unnamed x10 -> x16, local copies, waits for them, and re-layouts: 2.14 us -> 5.47 us
  transfers between devices with their start and end apart: 4 -> 4, of which waited for: 3 -> 3; matrix products, arithmetic and copies ran while one was open for 0% -> 0% of each run, Pallas kernels for 8% -> 7%
where the time goes in v2:
time: 238 us; the launch traced here: 237 us
  blocking collectives  137 us (58%)
  starting transfers between devices  37.3 us (16%)
  waiting for transfers between devices  29 us (12%)
  Pallas kernels  27.3 us (11%)
  local copies, waits for them, and re-layouts  5.47 us (2%)
    all_to_all x5, blocking collectives, exchange(): return lax.all_to_all(pieces, axis, 0, 0, tiled=True).reshape(x.shape)  91.3 us
    all_gather x3, blocking collectives, residual_of(): return lax.all_gather(mine, 'blk', tiled=True)  45.8 us
    all_to_all x4, starting transfers between devices, exchange(): return lax.all_to_all(pieces, axis, 0, 0, tiled=True).reshape(x.shape)  37.3 us
    all_to_all x4, waiting for transfers between devices, exchange(): return lax.all_to_all(pieces, axis, 0, 0, tiled=True).reshape(x.shape)  29 us
    pallas_call x14, Pallas kernels, call(): pl.pallas_call(kernel, out_shape=outs, in_specs=specs, out_specs=[pl.Bloc...  27.3 us
    unnamed x16, local copies, waits for them, and re-layouts  5.47 us
  transfers between devices with their start and end apart: 4, of which 3 were waited for; matrix products, arithmetic and copies ran while one was open for 0% of the time, Pallas kernels for 7%

profile of v2, /device:TPU:1, one launch (start us, length us, event | category | flops | bytes accessed | tf_op | source)
XLA Modules:
  0.0 237.0 jit_solution(3272802349245059483)
XLA Ops:
  0.6 0.0 copy-start.6
  0.6 0.7 copy-done.6
  1.3 0.0 copy-start.4
  1.3 1.1 copy-done.4
  2.4 0.0 copy-start.5
  2.4 1.0 copy-done.5
  3.4 4.2 %features.1 = (bf16[512,896]{1,0:T(8,128)(2,1)S(1)}, f32[1280,128]{1,0:T(8,128)}) custom-call(bf16[28,4,1792]{2,1,0:T(4,128)(2,1)S(1)} %bitcast.40, bf16[576,512]{1,0:T(8,128)(2,1)S(1)} %bitcast.39, f32[1,512]{1,0:T(1,128)S(1)} %bitcast.41), custom_call_target="tpu_custom_call" | custom-call | flops 2000000000 | bytes 2566144 | tf_op jit(solution)/shard_map/features/pallas_call | solution.py:60
  7.6 0.0 copy-start
  7.6 10.6 %all-to-all-start.2 = ((f32[32,40,128]{2,1,0:T(8,128)}), f32[32,40,128]{2,1,0:T(8,128)S(1)}, u32[]{:S(2)}, u32[]{:S(2)}) async-start(f32[32,40,128]{2,1,0:T(8,128)} %bitcast.10), calls=%async_computation.2 | async-start | bytes 1310720 | tf_op jit(solution)/shard_map/all_to_all | solution.py:301
  18.2 0.0 copy-done
  18.2 1.2 predict.3
  19.4 15.9 %all-to-all-done.2 = f32[32,40,128]{2,1,0:T(8,128)S(1)} async-done(((f32[32,40,128]{2,1,0:T(8,128)}), f32[32,40,128]{2,1,0:T(8,128)S(1)}, u32[]{:S(2)}, u32[]{:S(2)}) %all-to-all-start.2) | async-done | bytes 655392 | tf_op jit(solution)/shard_map/all_to_all | solution.py:301
  35.3 14.4 %all-to-all-start = ((bf16[16,72,128]{2,1,0:T(8,128)(2,1)}), bf16[16,72,128]{2,1,0:T(8,128)(2,1)S(1)}, u32[]{:S(2)}, u32[]{:S(2)}) async-start(bf16[16,72,128]{2,1,0:T(8,128)(2,1)} %bitcast.5), calls=%async_computation | async-start | bytes 589824 | tf_op jit(solution)/shard_map/all_to_all | solution.py:301
  49.6 0.9 gram.1
  50.6 11.4 %all-to-all-done = bf16[16,72,128]{2,1,0:T(8,128)(2,1)S(1)} async-done(((bf16[16,72,128]{2,1,0:T(8,128)(2,1)}), bf16[16,72,128]{2,1,0:T(8,128)(2,1)S(1)}, u32[]{:S(2)}, u32[]{:S(2)}) %all-to-all-start) | async-done | bytes 294944 | tf_op jit(solution)/shard_map/all_to_all | solution.py:301
  61.9 4.9 %all-to-all-start.3 = ((f32[32,40,128]{2,1,0:T(8,128)}), f32[32,40,128]{2,1,0:T(8,128)S(1)}, u32[]{:S(2)}, u32[]{:S(2)}) async-start(f32[32,40,128]{2,1,0:T(8,128)} %bitcast.12), calls=%async_computation.3 | async-start | bytes 1310720 | tf_op jit(solution)/shard_map/all_to_all | solution.py:301
  66.8 0.0 copy-start.7
  66.8 0.7 copy-done.7
  67.5 0.1 residual.3
  67.6 15.3 %all_gather.9.r_0_ = bf16[1152,128]{1,0:T(8,128)(2,1)S(1)} all-gather(bf16[72,128]{1,0:T(8,128)(2,1)S(1)} %residual.3), channel_id=1, replica_groups=mesh['img'=32,'blk'=16] {'blk'}, dimensions={0}, use_global_device_ids=true | all-gather | bytes 313344 | tf_op jit(solution)/shard_map/all_gather | solution.py:344
  82.8 1.2 project.2
  84.1 1.8 all-to-all-done.3
  85.9 0.0 copy-start.2
  85.9 7.5 %all-to-all-start.1 = ((f32[32,24,128]{2,1,0:T(8,128)}), f32[32,24,128]{2,1,0:T(8,128)S(1)}, u32[]{:S(2)}, u32[]{:S(2)}) async-start(f32[32,24,128]{2,1,0:T(8,128)} %bitcast.8), calls=%async_computation.1 | async-start | bytes 786432 | tf_op jit(solution)/shard_map/all_to_all | solution.py:301
  93.3 0.0 copy-done.2
  93.3 0.0 copy-start.3
  93.3 1.1 copy-done.3
  94.4 13.9 %inverse.1 = (bf16[1024,512]{1,0:T(8,128)(2,1)S(1)}, bf16[1024,512]{1,0:T(8,128)(2,1)S(1)}) custom-call(f32[1280,128]{1,0:T(8,128)S(1)} %bitcast.35), custom_call_target="tpu_custom_call" | custom-call | flops 14000000000 | bytes 2752512 | tf_op jit(solution)/shard_map/inverse/pallas_call | solution.py:60
  108.3 0.0 all-to-all-done.1
  108.3 0.0 copy-start.1
  108.3 1.0 copy-done.1
  109.3 1.2 solve.2
  110.5 18.4 %all_to_all.45 = bf16[32,24,128]{2,1,0:T(8,128)(2,1)S(1)} all-to-all(bf16[32,24,128]{2,1,0:T(8,128)(2,1)S(1)} %bitcast.38), channel_id=1, replica_groups=mesh['img'=32,'blk'=16] {'img'}, dimensions={0} | all-to-all | bytes 393216 | tf_op jit(solution)/shard_map/all_to_all | solution.py:301
  128.9 0.5 predict.4
  129.4 20.6 %all_to_all.46 = bf16[16,72,128]{2,1,0:T(8,128)(2,1)S(1)} all-to-all(bf16[16,72,128]{2,1,0:T(8,128)(2,1)S(1)} %bitcast.32), channel_id=1, replica_groups=mesh['img'=32,'blk'=16] {'blk'}, dimensions={0} | all-to-all | bytes 589824 | tf_op jit(solution)/shard_map/all_to_all | solution.py:301
  150.0 0.1 residual.4
  150.1 15.3 %all_gather.10.r_0_ = bf16[1152,128]{1,0:T(8,128)(2,1)S(1)} all-gather(bf16[72,128]{1,0:T(8,128)(2,1)S(1)} %residual.4), channel_id=1, replica_groups=mesh['img'=32,'blk'=16] {'blk'}, dimensions={0}, use_global_device_ids=true | all-gather | bytes 313344 | tf_op jit(solution)/shard_map/all_gather | solution.py:344
  165.3 0.5 project.3
  165.8 15.8 %all_to_all.47 = f32[32,24,128]{2,1,0:T(8,128)S(1)} all-to-all(f32[32,24,128]{2,1,0:T(8,128)S(1)} %bitcast.27), channel_id=1, replica_groups=mesh['img'=32,'blk'=16] {'img'}, dimensions={0} | all-to-all | bytes 786432 | tf_op jit(solution)/shard_map/all_to_all | solution.py:301
  181.6 1.8 solve.3
  183.4 16.7 %all_to_all.48 = bf16[32,24,128]{2,1,0:T(8,128)(2,1)S(1)} all-to-all(bf16[32,24,128]{2,1,0:T(8,128)(2,1)S(1)} %bitcast.37), channel_id=1, replica_groups=mesh['img'=32,'blk'=16] {'img'}, dimensions={0} | all-to-all | bytes 393216 | tf_op jit(solution)/shard_map/all_to_all | solution.py:301
  200.1 0.9 predict.5
  201.0 19.9 %all_to_all.49 = bf16[16,72,128]{2,1,0:T(8,128)(2,1)S(1)} all-to-all(bf16[16,72,128]{2,1,0:T(8,128)(2,1)S(1)} %bitcast.36), channel_id=1, replica_groups=mesh['img'=32,'blk'=16] {'blk'}, dimensions={0} | all-to-all | bytes 589824 | tf_op jit(solution)/shard_map/all_to_all | solution.py:301
  220.8 0.1 residual.5
  220.9 15.3 %all_gather.11.got = bf16[1152,128]{1,0:T(8,128)(2,1)S(1)} all-gather(bf16[72,128]{1,0:T(8,128)(2,1)S(1)} %residual.5), channel_id=1, replica_groups=mesh['img'=32,'blk'=16] {'blk'}, dimensions={0}, use_global_device_ids=true | all-gather | bytes 313344 | tf_op jit(solution)/shard_map/all_gather | solution.py:344
  236.2 0.8 output.1
  (1 shorter events, 0.0 us)
Async XLA Ops:
  0.6 0.7 copy-start.6
  1.3 1.1 copy-start.4
  2.4 1.0 copy-start.5
  7.6 10.6 %copy-start = (f32[150,512]{1,0:T(8,128)S(1)}, f32[150,512]{1,0:T(8,128)}, u32[]{:S(2)}) copy-start(f32[150,512]{1,0:T(8,128)} %r_2_.1) | copy-start | bytes 921604
  7.6 27.7 %all-to-all-start.2 = ((f32[32,40,128]{2,1,0:T(8,128)}), f32[32,40,128]{2,1,0:T(8,128)S(1)}, u32[]{:S(2)}, u32[]{:S(2)}) async-start(f32[32,40,128]{2,1,0:T(8,128)} %bitcast.10), calls=%async_computation.2 | async-start | bytes 1310720 | tf_op jit(solution)/shard_map/all_to_all | solution.py:301
  35.3 26.7 %all-to-all-start = ((bf16[16,72,128]{2,1,0:T(8,128)(2,1)}), bf16[16,72,128]{2,1,0:T(8,128)(2,1)S(1)}, u32[]{:S(2)}, u32[]{:S(2)}) async-start(bf16[16,72,128]{2,1,0:T(8,128)(2,1)} %bitcast.5), calls=%async_computation | async-start | bytes 589824 | tf_op jit(solution)/shard_map/all_to_all | solution.py:301
  61.9 23.9 %all-to-all-start.3 = ((f32[32,40,128]{2,1,0:T(8,128)}), f32[32,40,128]{2,1,0:T(8,128)S(1)}, u32[]{:S(2)}, u32[]{:S(2)}) async-start(f32[32,40,128]{2,1,0:T(8,128)} %bitcast.12), calls=%async_computation.3 | async-start | bytes 1310720 | tf_op jit(solution)/shard_map/all_to_all | solution.py:301
  66.8 0.7 copy-start.7
  85.9 7.5 %copy-start.2 = (f32[32,40,128]{2,1,0:T(8,128)}, f32[32,40,128]{2,1,0:T(8,128)S(1)}, u32[]{:S(2)}) copy-start(f32[32,40,128]{2,1,0:T(8,128)S(1)} %all-to-all-done.3) | copy-start | bytes 1966084
  85.9 22.5 %all-to-all-start.1 = ((f32[32,24,128]{2,1,0:T(8,128)}), f32[32,24,128]{2,1,0:T(8,128)S(1)}, u32[]{:S(2)}, u32[]{:S(2)}) async-start(f32[32,24,128]{2,1,0:T(8,128)} %bitcast.8), calls=%async_computation.1 | async-start | bytes 786432 | tf_op jit(solution)/shard_map/all_to_all | solution.py:301
  93.3 1.1 copy-start.3
  108.3 1.0 copy-start.1

commit v3 on v2

--- a/solution.py
+++ b/solution.py
@@ -7,6 +7,7 @@
 from jax.experimental import pallas as pl
 from jax.experimental.pallas import tpu as pltpu
 from jax.sharding import PartitionSpec as P
+
 
 SIDE = 28
 CHAN = 64
@@ -51,7 +52,7 @@
     return -(-n // 8) * 8
 
 
-def call(kernel, outs, *args, scratch=(), name=None, flops=0):
+def call(kernel, outs, *args, scratch=(), flops=0):
     specs = [
         pl.BlockSpec(memory_space=pltpu.SMEM if a.dtype == jnp.int32 and a.ndim == 1 else pltpu.VMEM)
         for a in args
@@ -64,7 +65,6 @@
         out_specs=[pl.BlockSpec(memory_space=pltpu.VMEM)] * len(outs),
         scratch_shapes=scratch,
         compiler_params=pltpu.CompilerParams(vmem_limit_bytes=20 * 2**20),
-        name=name,
         cost_estimate=pl.CostEstimate(flops=flops, bytes_accessed=size, transcendentals=0),
     )(*args)
 
@@ -76,10 +76,10 @@
 def store_prediction(stack_ref, weights, features, shrink):
     for t in range(features.shape[1] // TILE):
         part = jnp.dot(weights, features[:, t * TILE : (t + 1) * TILE], preferred_element_type=F32)
-        stack_ref[t * ROWS : (t + 1) * ROWS] = (part * shrink).astype(BF16)
+        stack_ref[t * ROWS : (t + 1) * ROWS] = (part * shrink).astype(BF16).astype(stack_ref.dtype)
     used = features.shape[1] // TILE * ROWS
     if used < stack_ref.shape[0]:
-        stack_ref[used:] = jnp.zeros((stack_ref.shape[0] - used, TILE), BF16)
+        stack_ref[used:] = jnp.zeros((stack_ref.shape[0] - used, TILE), stack_ref.dtype)
 
 
 def feature_kernel(img, filt, phase, feat, gram, rows32, patches, taps):
@@ -123,10 +123,27 @@
             at += TILE
 
 
-def first_predict_kernel(shrink, weights, feat, stack, wide):
+def bit_of(place, level):
+    return jnp.bitwise_and(jnp.right_shift(place[0], level), 1)
+
+
+def halved(place, level, whole, send, keep):
+    half = keep.shape[0]
+    mine = bit_of(place, level)
+    send[...] = whole[pl.ds(pl.multiple_of((1 - mine) * half, 8), half), :].astype(BF16)
+    keep[...] = whole[pl.ds(pl.multiple_of(mine * half, 8), half), :]
+
+
+def first_predict_kernel(shrink, place, weights, feat, send, keep, wide, whole):
     wide[...] = jnp.zeros_like(wide)
     wide[:LABELS] = weights[...]
-    store_prediction(stack, wide[...].astype(BF16), feat[...], shrink)
+    store_prediction(whole, wide[...].astype(BF16), feat[...], shrink)
+    halved(place, 0, whole, send, keep)
+
+
+def halving_kernel(level, place, got, kept, send, keep, whole):
+    whole[...] = kept[...] + got[...].astype(F32)
+    halved(place, level, whole, send, keep)
 
 
 def summed(ref, parts):
@@ -143,14 +160,23 @@
         ref[k * rows : (k + 1) * rows] = value
 
 
-def residual_kernel(parts, place, got, labels, out):
-    total = summed(got, parts)
-    rows = total.shape[0]
-    line = lax.broadcasted_iota(jnp.int32, total.shape, 0) + place[0] * rows
+def rest(total, first, labels):
+    line = lax.broadcasted_iota(jnp.int32, total.shape, 0) + first
     targets = jnp.zeros_like(total)
     for t in range(labels.shape[0]):
         targets += jnp.where(line - t * ROWS == labels[t : t + 1], 1.0, 0.0)
-    out[...] = (targets - total).astype(BF16)
+    return (targets - total).astype(BF16)
+
+
+def residual_kernel(parts, place, got, labels, out):
+    out[...] = rest(summed(got, parts), place[0] * out.shape[0], labels)
+
+
+def first_residual_kernel(levels, place, got, kept, labels, out):
+    segment = 0
+    for level in range(levels):
+        segment = segment * 2 + bit_of(place, level)
+    out[...] = rest(kept[...] + got[...].astype(F32), segment * out.shape[0], labels)
 
 
 def gram_kernel(parts, got, out):
@@ -161,9 +187,15 @@
     return jnp.concatenate([ref[t * ROWS : (t + 1) * ROWS] for t in range(tiles)], axis=1)
 
 
-def project_kernel(parts, got, feat, out, spread):
+def project_kernel(parts, order, got, feat, out, spread, flat):
     tiles = feat.shape[1] // TILE
-    projected = contract_last(unstacked(got, tiles), feat[...])
+    source = got
+    if order is not None:
+        rows = got.shape[0] // len(order)
+        for k, at in enumerate(order):
+            flat[at * rows : (at + 1) * rows] = got[k * rows : (k + 1) * rows]
+        source = flat
+    projected = contract_last(unstacked(source, tiles), feat[...])
     own = ROWS // parts
     rows = spread.shape[0] // parts
     lanes = FILT // TILE
@@ -329,55 +361,78 @@
             pltpu.VMEM((DEEP // PAIR, padded, PAIR), F32),
             pltpu.VMEM((DEEP, FILT), BF16),
         ],
-        name="features", flops=2 * 10**9,
-    )
-    (stack,) = call(
-        lambda *r: first_predict_kernel(shrink, *r), [shape(stack_rows, TILE, dtype=BF16)], weights, feat,
-        scratch=[pltpu.VMEM((ROWS, FILT), F32)], name="predict", flops=10**8,
-    )
+        flops=2 * 10**9,
+    )
+    levels = blocks.bit_length() - 1
+    order = [sum((k >> level & 1) << (levels - 1 - level) for level in range(levels)) for k in range(blocks)]
+
+    def halves(level):
+        rows = stack_rows >> (level + 1)
+        return [shape(rows, TILE, dtype=BF16), shape(rows, TILE)]
+
+    def swapped(send, level):
+        pairs = [(k, k ^ (1 << level)) for k in range(blocks)]
+        return lax.ppermute(send, "blk", pairs)
+
+    def first_residual():
+        send, keep = call(
+            lambda *r: first_predict_kernel(shrink, *r), halves(0), blk_place, weights, feat,
+            scratch=[pltpu.VMEM((ROWS, FILT), F32), pltpu.VMEM((stack_rows, TILE), F32)],
+            flops=10**8,
+        )
+        for level in range(1, levels):
+            send, keep = call(
+                lambda *r: halving_kernel(level, *r), halves(level),
+                blk_place, swapped(send, level - 1), keep,
+                scratch=[pltpu.VMEM((stack_rows >> level, TILE), F32)],
+            )
+        (mine,) = call(
+            lambda *r: first_residual_kernel(levels, *r), [shape(stack_rows // blocks, TILE, dtype=BF16)],
+            blk_place, swapped(send, levels - 1), keep, label_tiles,
+        )
+        return lax.all_gather(mine, "blk", tiled=True)
 
     def residual_of(stack):
         (mine,) = call(
             lambda *r: residual_kernel(blocks, *r), [shape(stack_rows // blocks, TILE, dtype=BF16)],
-            blk_place, exchange(stack, "blk"), label_tiles, name="residual",
+            blk_place, exchange(stack, "blk"), label_tiles,
         )
         return lax.all_gather(mine, "blk", tiled=True)
 
-    def projection_of(residual):
+    def projection_of(residual, order):
         (parts,) = call(
-            lambda *r: project_kernel(groups, *r), [shape(fold_rows, TILE)],
-            residual, feat, scratch=[pltpu.VMEM((fold_rows, TILE), F32)], name="project", flops=10**8,
+            lambda *r: project_kernel(groups, order, *r), [shape(fold_rows, TILE)], residual, feat,
+            scratch=[pltpu.VMEM((fold_rows, TILE), F32), pltpu.VMEM((stack_rows, TILE), BF16)],
+            flops=10**8,
         )
         return exchange(parts, "img")
 
-    residual = residual_of(stack)
-    (gram_sum,) = call(
-        lambda *r: gram_kernel(groups, *r), [shape(gram_rows, TILE)], exchange(gram_part, "img"), name="gram",
-    )
+    residual = first_residual()
+    (gram_sum,) = call(lambda *r: gram_kernel(groups, *r), [shape(gram_rows, TILE)], exchange(gram_part, "img"))
     matrix, inverse = call(
         lambda *r: inverse_kernel(ridge, *r), [shape(2 * FILT, FILT, dtype=BF16)] * 2,
         exchange(gram_sum, "img"),
         scratch=[pltpu.VMEM((FILT, 3 * FILT), BF16), pltpu.VMEM((FILT, FILT), F32)],
-        name="inverse", flops=14 * 10**9,
+        flops=14 * 10**9,
     )
     own = weights
     for step in range(ITERS):
         last = step == ITERS - 1
-        projected = projection_of(residual)
+        projected = projection_of(residual, None if step else order)
         own, spread = call(
             lambda *r: solve_kernel(groups, factor, *r), [shape(tall, FILT), shape(fold_rows, TILE, dtype=BF16)],
             img_place, projected, own, matrix, inverse,
             scratch=[pltpu.VMEM((tall * (FILT // TILE), TILE), F32), pltpu.VMEM((ROWS, FILT), F32)],
-            name="solve", flops=10**8,
+            flops=10**8,
         )
         found = call(
             lambda *r: predict_kernel(groups, shrink, last, *r),
             [shape(stack_rows, TILE, dtype=BF16)] + ([shape(LABELS, FILT)] if last else []),
             exchange(spread, "img"), feat,
-            scratch=[pltpu.VMEM((fold_rows, TILE), F32)], name="predict", flops=10**8,
+            scratch=[pltpu.VMEM((fold_rows, TILE), F32)], flops=10**8,
         )
         residual = residual_of(found[0])
-    (out,) = call(output_kernel, [shape(LABELS, here)], residual, name="output")
+    (out,) = call(output_kernel, [shape(LABELS, here)], residual)
     return (found[1], out)
 
 

time: 238 us -> 247 us (1.038)
  blocking collectives: 137 us -> 170 us
  waiting for transfers between devices: 29 us -> 6.01 us
    all_to_all x4 -> x2, waiting for transfers between devices: 29 us -> 0.01 us  [exchange(): return lax.all_to_all(pieces, axis, 0, 0, tiled=True).reshape(x.shape)]
    all_to_all x5 -> x6, blocking collectives: 91.3 us -> 116 us  [exchange(): return lax.all_to_all(pieces, axis, 0, 0, tiled=True).reshape(x.shape)]
    all_gather x0 -> x1, blocking collectives: none -> 24 us  [first_residual(): return lax.all_gather(mine, 'blk', tiled=True)]
    ppermute x0 -> x4, starting transfers between devices: none -> 21.4 us  [swapped(): return lax.ppermute(send, 'blk', pairs)]
    all_to_all x4 -> x2, starting transfers between devices: 37.3 us -> 17.4 us  [exchange(): return lax.all_to_all(pieces, axis, 0, 0, tiled=True).reshape(x.shape)]
    all_gather x3 -> x2, blocking collectives: 45.8 us -> 30.5 us  [residual_of(): return lax.all_gather(mine, 'blk', tiled=True)]
    ppermute x0 -> x4, waiting for transfers between devices: none -> 6 us  [swapped(): return lax.ppermute(send, 'blk', pairs)]
    pallas_call x14 -> x17, Pallas kernels: 27.3 us -> 25.9 us  [call(): pl.pallas_call(kernel, out_shape=outs, in_specs=specs, out_specs=[pl.Bloc...]
  transfers between devices with their start and end apart: 4 -> 6, of which waited for: 3 -> 4; matrix products, arithmetic and copies ran while one was open for 0% -> 0% of each run, Pallas kernels for 7% -> 6%
where the time goes in v3:
time: 247 us
  blocking collectives  170 us (69%)
  starting transfers between devices  38.7 us (16%)
  Pallas kernels  25.9 us (10%)
  waiting for transfers between devices  6.01 us (2%)
  local copies, waits for them, and re-layouts  4.79 us (2%)
    all_to_all x6, blocking collectives, exchange(): return lax.all_to_all(pieces, axis, 0, 0, tiled=True).reshape(x.shape)  116 us
    all_gather x2, blocking collectives, residual_of(): return lax.all_gather(mine, 'blk', tiled=True)  30.5 us
    pallas_call x17, Pallas kernels, call(): pl.pallas_call(kernel, out_shape=outs, in_specs=specs, out_specs=[pl.Bloc...  25.9 us
    all_gather x1, blocking collectives, first_residual(): return lax.all_gather(mine, 'blk', tiled=True)  24 us
    ppermute x4, starting transfers between devices, swapped(): return lax.ppermute(send, 'blk', pairs)  21.4 us
    all_to_all x2, starting transfers between devices, exchange(): return lax.all_to_all(pieces, axis, 0, 0, tiled=True).reshape(x.shape)  17.4 us
    ppermute x4, waiting for transfers between devices, swapped(): return lax.ppermute(send, 'blk', pairs)  6 us
  transfers between devices with their start and end apart: 6, of which 4 were waited for; matrix products, arithmetic and copies ran while one was open for 0% of the time, Pallas kernels for 6%

profile of v3, /device:TPU:1, one launch (start us, length us, event | category | flops | bytes accessed | tf_op | source)
XLA Modules:
  0.0 246.6 jit_solution(16703977967897831076)
XLA Ops:
  0.6 0.0 copy-start.6
  0.6 0.7 copy-done.6
  1.3 0.0 copy-start.4
  1.3 1.1 copy-done.4
  2.4 0.0 copy-start.5
  2.4 1.0 copy-done.5
  3.4 3.3 %shard_map.68 = (bf16[512,896]{1,0:T(8,128)(2,1)S(1)}, f32[1280,128]{1,0:T(8,128)S(1)}) custom-call(bf16[28,4,1792]{2,1,0:T(4,128)(2,1)S(1)} %bitcast.38, bf16[576,512]{1,0:T(8,128)(2,1)S(1)} %bitcast.37, f32[1,512]{1,0:T(1,128)S(1)} %bitcast.39), custom_call_target="tpu_custom_call" | custom-call | flops 2000000000 | bytes 2566144 | tf_op jit(solution)/shard_map/pallas_call | solution.py:61
  6.7 27.3 %all_to_all.40 = f32[32,40,128]{2,1,0:T(8,128)S(1)} all-to-all(f32[32,40,128]{2,1,0:T(8,128)S(1)} %bitcast.33), channel_id=1, replica_groups=mesh['img'=32,'blk'=16] {'img'}, dimensions={0} | all-to-all | bytes 1310720 | tf_op jit(solution)/shard_map/all_to_all | solution.py:333
  34.1 0.9 shard_map.75
  35.0 0.0 copy-start
  35.0 7.9 %all-to-all-start.2 = ((f32[32,40,128]{2,1,0:T(8,128)}), f32[32,40,128]{2,1,0:T(8,128)S(1)}, u32[]{:S(2)}, u32[]{:S(2)}) async-start(f32[32,40,128]{2,1,0:T(8,128)} %bitcast.10), calls=%async_computation.2 | async-start | bytes 1310720 | tf_op jit(solution)/shard_map/all_to_all | solution.py:333
  42.9 0.0 copy-done
  42.9 0.5 shard_map.69
  43.4 3.4 %collective-permute-start = (bf16[576,128]{1,0:T(8,128)(2,1)S(1)}, bf16[576,128]{1,0:T(8,128)(2,1)S(1)}, u32[]{:S(2)}, u32[]{:S(2)}) collective-permute-start(bf16[576,128]{1,0:T(8,128)(2,1)S(1)} %get-tuple-element.20), channel_id=1, source_target_pairs={{0,1},{1,0},{2,3},{3,2},{4,5},{5,4},{6,7},{7,6},{8,9},{9,8},{10,11... | collective-permute-start | bytes 442376 | tf_op jit(solution)/shard_map/ppermute | solution.py:375
  46.8 1.0 collective-permute-done.r_1_
  47.8 0.1 shard_map.70
  47.9 4.0 %collective-permute-start.1 = (bf16[288,128]{1,0:T(8,128)(2,1)S(1)}, bf16[288,128]{1,0:T(8,128)(2,1)S(1)}, u32[]{:S(2)}, u32[]{:S(2)}) collective-permute-start(bf16[288,128]{1,0:T(8,128)(2,1)S(1)} %get-tuple-element.22), channel_id=1, source_target_pairs={{0,2},{1,3},{2,0},{3,1},{4,6},{5,7},{6,4},{7,5},{8,10},{9,11},{10,... | collective-permute-start | bytes 221192 | tf_op jit(solution)/shard_map/ppermute | solution.py:375
  51.9 2.3 collective-permute-done.1.r_1_
  54.1 0.0 copy-start.7
  54.2 5.8 %collective-permute-start.2 = (bf16[144,128]{1,0:T(8,128)(2,1)S(1)}, bf16[144,128]{1,0:T(8,128)(2,1)S(1)}, u32[]{:S(2)}, u32[]{:S(2)}) collective-permute-start(bf16[144,128]{1,0:T(8,128)(2,1)S(1)} %get-tuple-element.24), channel_id=1, source_target_pairs={{0,4},{1,5},{2,6},{3,7},{4,0},{5,1},{6,2},{7,3},{8,12},{9,13},{10,... | collective-permute-start | bytes 110600 | tf_op jit(solution)/shard_map/ppermute | solution.py:375
  60.0 1.6 collective-permute-done.2.r_1_
  61.6 8.2 %collective-permute-start.3 = (bf16[72,128]{1,0:T(8,128)(2,1)S(1)}, bf16[72,128]{1,0:T(8,128)(2,1)S(1)}, u32[]{:S(2)}, u32[]{:S(2)}) collective-permute-start(bf16[72,128]{1,0:T(8,128)(2,1)S(1)} %get-tuple-element.26), channel_id=1, source_target_pairs={{0,8},{1,9},{2,10},{3,11},{4,12},{5,13},{6,14},{7,15},{8,0},{9,1},... | collective-permute-start | bytes 55304 | tf_op jit(solution)/shard_map/ppermute | solution.py:375
  69.8 0.0 copy-done.7
  69.9 1.1 collective-permute-done.3.r_1_
  71.0 24.0 %all_gather.9.r_0_ = bf16[1152,128]{1,0:T(8,128)(2,1)S(1)} all-gather(bf16[72,128]{1,0:T(8,128)(2,1)S(1)} %shard_map.73), channel_id=1, replica_groups=mesh['img'=32,'blk'=16] {'blk'}, dimensions={0}, use_global_device_ids=true | all-gather | bytes 313344 | tf_op jit(solution)/shard_map/all_gather | solution.py:393
  95.1 1.2 shard_map.74
  96.3 0.0 all-to-all-done.2
  96.3 0.0 copy-start.2
  96.3 9.5 %all-to-all-start = ((f32[32,24,128]{2,1,0:T(8,128)}), f32[32,24,128]{2,1,0:T(8,128)S(1)}, u32[]{:S(2)}, u32[]{:S(2)}) async-start(f32[32,24,128]{2,1,0:T(8,128)} %bitcast.6), calls=%async_computation | async-start | bytes 786432 | tf_op jit(solution)/shard_map/all_to_all | solution.py:333
  105.8 0.0 copy-done.2
  105.8 0.0 copy-start.3
  105.8 1.1 copy-done.3
  106.9 13.9 %shard_map.76 = (bf16[1024,512]{1,0:T(8,128)(2,1)S(1)}, bf16[1024,512]{1,0:T(8,128)(2,1)S(1)}) custom-call(f32[1280,128]{1,0:T(8,128)S(1)} %bitcast.32), custom_call_target="tpu_custom_call" | custom-call | flops 14000000000 | bytes 2752512 | tf_op jit(solution)/shard_map/pallas_call | solution.py:61
  120.8 0.0 all-to-all-done
  120.8 0.0 copy-start.1
  120.9 1.0 copy-done.1
  121.8 1.2 shard_map.77
  123.0 18.4 %all_to_all.41 = bf16[32,24,128]{2,1,0:T(8,128)(2,1)S(1)} all-to-all(bf16[32,24,128]{2,1,0:T(8,128)(2,1)S(1)} %bitcast.36), channel_id=1, replica_groups=mesh['img'=32,'blk'=16] {'img'}, dimensions={0} | all-to-all | bytes 393216 | tf_op jit(solution)/shard_map/all_to_all | solution.py:333
  141.4 0.5 shard_map.78
  141.9 17.9 %all_to_all.42 = bf16[16,72,128]{2,1,0:T(8,128)(2,1)S(1)} all-to-all(bf16[16,72,128]{2,1,0:T(8,128)(2,1)S(1)} %bitcast.29), channel_id=1, replica_groups=mesh['img'=32,'blk'=16] {'blk'}, dimensions={0} | all-to-all | bytes 589824 | tf_op jit(solution)/shard_map/all_to_all | solution.py:333
  159.8 0.1 shard_map.79
  159.9 15.3 %all_gather.10.r_0_ = bf16[1152,128]{1,0:T(8,128)(2,1)S(1)} all-gather(bf16[72,128]{1,0:T(8,128)(2,1)S(1)} %shard_map.79), channel_id=1, replica_groups=mesh['img'=32,'blk'=16] {'blk'}, dimensions={0}, use_global_device_ids=true | all-gather | bytes 313344 | tf_op jit(solution)/shard_map/all_gather | solution.py:400
  175.1 0.5 shard_map.80
  175.6 15.8 %all_to_all.43 = f32[32,24,128]{2,1,0:T(8,128)S(1)} all-to-all(f32[32,24,128]{2,1,0:T(8,128)S(1)} %bitcast.25), channel_id=1, replica_groups=mesh['img'=32,'blk'=16] {'img'}, dimensions={0} | all-to-all | bytes 786432 | tf_op jit(solution)/shard_map/all_to_all | solution.py:333
  191.4 1.8 shard_map.81
  193.2 16.7 %all_to_all.44 = bf16[32,24,128]{2,1,0:T(8,128)(2,1)S(1)} all-to-all(bf16[32,24,128]{2,1,0:T(8,128)(2,1)S(1)} %bitcast.35), channel_id=1, replica_groups=mesh['img'=32,'blk'=16] {'img'}, dimensions={0} | all-to-all | bytes 393216 | tf_op jit(solution)/shard_map/all_to_all | solution.py:333
  209.9 0.9 shard_map.82
  210.8 19.6 %all_to_all.45 = bf16[16,72,128]{2,1,0:T(8,128)(2,1)S(1)} all-to-all(bf16[16,72,128]{2,1,0:T(8,128)(2,1)S(1)} %bitcast.34), channel_id=1, replica_groups=mesh['img'=32,'blk'=16] {'blk'}, dimensions={0} | all-to-all | bytes 589824 | tf_op jit(solution)/shard_map/all_to_all | solution.py:333
  230.4 0.1 shard_map.83
  230.5 15.3 %all_gather.11.got = bf16[1152,128]{1,0:T(8,128)(2,1)S(1)} all-gather(bf16[72,128]{1,0:T(8,128)(2,1)S(1)} %shard_map.83), channel_id=1, replica_groups=mesh['img'=32,'blk'=16] {'blk'}, dimensions={0}, use_global_device_ids=true | all-gather | bytes 313344 | tf_op jit(solution)/shard_map/all_gather | solution.py:400
  245.7 0.8 shard_map.84
  (4 shorter events, 0.1 us)
Async XLA Ops:
  0.6 0.7 copy-start.6
  1.3 1.1 copy-start.4
  2.4 1.0 copy-start.5
  35.0 7.9 %copy-start = (f32[150,512]{1,0:T(8,128)S(1)}, f32[150,512]{1,0:T(8,128)}, u32[]{:S(2)}) copy-start(f32[150,512]{1,0:T(8,128)} %r_2_.1) | copy-start | bytes 921604
  35.0 61.3 %all-to-all-start.2 = ((f32[32,40,128]{2,1,0:T(8,128)}), f32[32,40,128]{2,1,0:T(8,128)S(1)}, u32[]{:S(2)}, u32[]{:S(2)}) async-start(f32[32,40,128]{2,1,0:T(8,128)} %bitcast.10), calls=%async_computation.2 | async-start | bytes 1310720 | tf_op jit(solution)/shard_map/all_to_all | solution.py:333
  43.4 4.4 %collective-permute-start = (bf16[576,128]{1,0:T(8,128)(2,1)S(1)}, bf16[576,128]{1,0:T(8,128)(2,1)S(1)}, u32[]{:S(2)}, u32[]{:S(2)}) collective-permute-start(bf16[576,128]{1,0:T(8,128)(2,1)S(1)} %get-tuple-element.20), channel_id=1, source_target_pairs={{0,1},{1,0},{2,3},{3,2},{4,5},{5,4},{6,7},{7,6},{8,9},{9,8},{10,11... | collective-permute-start | bytes 442376 | tf_op jit(solution)/shard_map/ppermute | solution.py:375
  47.9 6.3 %collective-permute-start.1 = (bf16[288,128]{1,0:T(8,128)(2,1)S(1)}, bf16[288,128]{1,0:T(8,128)(2,1)S(1)}, u32[]{:S(2)}, u32[]{:S(2)}) collective-permute-start(bf16[288,128]{1,0:T(8,128)(2,1)S(1)} %get-tuple-element.22), channel_id=1, source_target_pairs={{0,2},{1,3},{2,0},{3,1},{4,6},{5,7},{6,4},{7,5},{8,10},{9,11},{10,... | collective-permute-start | bytes 221192 | tf_op jit(solution)/shard_map/ppermute | solution.py:375
  54.1 15.7 %copy-start.7 = (s32[784]{0:T(1024)S(1)}, s32[784]{0:T(1024)}, u32[]{:S(2)}) copy-start(s32[784]{0:T(1024)} %param.8) | copy-start | bytes 9412
  54.2 7.4 %collective-permute-start.2 = (bf16[144,128]{1,0:T(8,128)(2,1)S(1)}, bf16[144,128]{1,0:T(8,128)(2,1)S(1)}, u32[]{:S(2)}, u32[]{:S(2)}) collective-permute-start(bf16[144,128]{1,0:T(8,128)(2,1)S(1)} %get-tuple-element.24), channel_id=1, source_target_pairs={{0,4},{1,5},{2,6},{3,7},{4,0},{5,1},{6,2},{7,3},{8,12},{9,13},{10,... | collective-permute-start | bytes 110600 | tf_op jit(solution)/shard_map/ppermute | solution.py:375
  61.6 9.4 %collective-permute-start.3 = (bf16[72,128]{1,0:T(8,128)(2,1)S(1)}, bf16[72,128]{1,0:T(8,128)(2,1)S(1)}, u32[]{:S(2)}, u32[]{:S(2)}) collective-permute-start(bf16[72,128]{1,0:T(8,128)(2,1)S(1)} %get-tuple-element.26), channel_id=1, source_target_pairs={{0,8},{1,9},{2,10},{3,11},{4,12},{5,13},{6,14},{7,15},{8,0},{9,1},... | collective-permute-start | bytes 55304 | tf_op jit(solution)/shard_map/ppermute | solution.py:375
  96.3 9.5 %copy-start.2 = (f32[32,40,128]{2,1,0:T(8,128)}, f32[32,40,128]{2,1,0:T(8,128)S(1)}, u32[]{:S(2)}) copy-start(f32[32,40,128]{2,1,0:T(8,128)S(1)} %all-to-all-done.2) | copy-start | bytes 1966084
  96.3 24.5 %all-to-all-start = ((f32[32,24,128]{2,1,0:T(8,128)}), f32[32,24,128]{2,1,0:T(8,128)S(1)}, u32[]{:S(2)}, u32[]{:S(2)}) async-start(f32[32,24,128]{2,1,0:T(8,128)} %bitcast.6), calls=%async_computation | async-start | bytes 786432 | tf_op jit(solution)/shard_map/all_to_all | solution.py:333
  105.8 1.1 copy-start.3
  120.8 1.0 copy-start.1

commit v4 on v2

--- a/solution.py
+++ b/solution.py
@@ -143,10 +143,17 @@
         ref[k * rows : (k + 1) * rows] = value
 
 
+def chip_kernel(place, both, out):
+    half = out.shape[0]
+    first = pl.multiple_of(jnp.bitwise_and(place[0], 1) * half, 16)
+    total = both[pl.ds(first, half), :].astype(F32) + both[pl.ds(first + 2 * half, half), :].astype(F32)
+    out[...] = total.astype(BF16)
+
+
 def residual_kernel(parts, place, got, labels, out):
     total = summed(got, parts)
-    rows = total.shape[0]
-    line = lax.broadcasted_iota(jnp.int32, total.shape, 0) + place[0] * rows
+    segment = jnp.bitwise_and(place[0], 1) * parts + jnp.right_shift(place[0], 1)
+    line = lax.broadcasted_iota(jnp.int32, total.shape, 0) + segment * total.shape[0]
     targets = jnp.zeros_like(total)
     for t in range(labels.shape[0]):
         targets += jnp.where(line - t * ROWS == labels[t : t + 1], 1.0, 0.0)
@@ -157,13 +164,21 @@
     copies(out, summed(got, parts), parts)
 
 
+def ordered(got, flat, blocks):
+    rows = got.shape[0] // blocks
+    for k in range(blocks):
+        at = (k % 2) * (blocks // 2) + k // 2
+        flat[at * rows : (at + 1) * rows] = got[k * rows : (k + 1) * rows]
+
+
 def unstacked(ref, tiles):
     return jnp.concatenate([ref[t * ROWS : (t + 1) * ROWS] for t in range(tiles)], axis=1)
 
 
-def project_kernel(parts, got, feat, out, spread):
+def project_kernel(parts, blocks, got, feat, out, spread, flat):
     tiles = feat.shape[1] // TILE
-    projected = contract_last(unstacked(got, tiles), feat[...])
+    ordered(got, flat, blocks)
+    projected = contract_last(unstacked(flat, tiles), feat[...])
     own = ROWS // parts
     rows = spread.shape[0] // parts
     lanes = FILT // TILE
@@ -288,11 +303,12 @@
     store_prediction(stack, weights.astype(BF16), feat[...], shrink)
 
 
-def output_kernel(got, out):
+def output_kernel(blocks, got, out, flat):
     tiles = -(-out.shape[1] // TILE)
+    ordered(got, flat, blocks)
     for t in range(tiles):
         wide = min(TILE, out.shape[1] - t * TILE)
-        out[:, t * TILE : t * TILE + wide] = got[t * ROWS : t * ROWS + LABELS, :wide].astype(F32)
+        out[:, t * TILE : t * TILE + wide] = flat[t * ROWS : t * ROWS + LABELS, :wide].astype(F32)
 
 
 def exchange(x, axis):
@@ -337,16 +353,25 @@
     )
 
     def residual_of(stack):
+        pairs = [[2 * k, 2 * k + 1] for k in range(blocks // 2)]
+        columns = [list(range(core, blocks, 2)) for core in range(2)]
+        both = lax.all_gather(stack, "blk", axis_index_groups=pairs, tiled=True)
+        (half,) = call(
+            chip_kernel, [shape(stack_rows // 2, TILE, dtype=BF16)], blk_place, both, name="chip",
+        )
+        pieces = half.reshape(blocks // 2, stack_rows // blocks, TILE)
+        got = lax.all_to_all(pieces, "blk", 0, 0, tiled=True, axis_index_groups=columns)
         (mine,) = call(
-            lambda *r: residual_kernel(blocks, *r), [shape(stack_rows // blocks, TILE, dtype=BF16)],
-            blk_place, exchange(stack, "blk"), label_tiles, name="residual",
+            lambda *r: residual_kernel(blocks // 2, *r), [shape(stack_rows // blocks, TILE, dtype=BF16)],
+            blk_place, got.reshape(half.shape), label_tiles, name="residual",
         )
         return lax.all_gather(mine, "blk", tiled=True)
 
     def projection_of(residual):
         (parts,) = call(
-            lambda *r: project_kernel(groups, *r), [shape(fold_rows, TILE)],
-            residual, feat, scratch=[pltpu.VMEM((fold_rows, TILE), F32)], name="project", flops=10**8,
+            lambda *r: project_kernel(groups, blocks, *r), [shape(fold_rows, TILE)], residual, feat,
+            scratch=[pltpu.VMEM((fold_rows, TILE), F32), pltpu.VMEM((stack_rows, TILE), BF16)],
+            name="project", flops=10**8,
         )
         return exchange(parts, "img")
 
@@ -377,7 +402,10 @@
             scratch=[pltpu.VMEM((fold_rows, TILE), F32)], name="predict", flops=10**8,
         )
         residual = residual_of(found[0])
-    (out,) = call(output_kernel, [shape(LABELS, here)], residual, name="output")
+    (out,) = call(
+        lambda *r: output_kernel(blocks, *r), [shape(LABELS, here)], residual,
+        scratch=[pltpu.VMEM((stack_rows, TILE), BF16)], name="output",
+    )
     return (found[1], out)
 
 

time: 238 us -> 232 us (0.975)
  waiting for transfers between devices: 29 us -> 20.3 us
    all_to_all x5 -> x3, blocking collectives: 91.3 us -> 50.9 us  [exchange(): return lax.all_to_all(pieces, axis, 0, 0, tiled=True).reshape(x.shape)]
    all_to_all x0 -> x2, blocking collectives: none -> 23.1 us  [residual_of(): lax.all_to_all(pieces, 'blk', 0, 0, tiled=True, axis_index_groups=columns)]
    all_to_all x4 -> x3, waiting for transfers between devices: 29 us -> 13.1 us  [exchange(): return lax.all_to_all(pieces, axis, 0, 0, tiled=True).reshape(x.shape)]
    all_gather x0 -> x3, blocking collectives: none -> 12.1 us  [residual_of(): both = lax.all_gather(stack, 'blk', axis_index_groups=pairs, tiled=True)]
    all_to_all x0 -> x1, starting transfers between devices: none -> 10 us  [residual_of(): lax.all_to_all(pieces, 'blk', 0, 0, tiled=True, axis_index_groups=columns)]
    all_to_all x4 -> x3, starting transfers between devices: 37.3 us -> 27.8 us  [exchange(): return lax.all_to_all(pieces, axis, 0, 0, tiled=True).reshape(x.shape)]
    all_to_all x0 -> x1, waiting for transfers between devices: none -> 7.18 us  [residual_of(): lax.all_to_all(pieces, 'blk', 0, 0, tiled=True, axis_index_groups=columns)]
    all_gather x3, blocking collectives: 45.8 us -> 52.9 us  [residual_of(): return lax.all_gather(mine, 'blk', tiled=True)]
  transfers between devices with their start and end apart: 4 -> 4, of which waited for: 3 -> 2; matrix products, arithmetic and copies ran while one was open for 0% -> 0% of each run, Pallas kernels for 7% -> 7%
where the time goes in v4:
time: 232 us; the launch traced here: 231 us
  blocking collectives  139 us (60%)
  starting transfers between devices  37.9 us (16%)
  Pallas kernels  27.3 us (12%)
  waiting for transfers between devices  20.3 us (9%)
  local copies, waits for them, and re-layouts  5.47 us (2%)
    all_gather x3, blocking collectives, residual_of(): return lax.all_gather(mine, 'blk', tiled=True)  52.9 us
    all_to_all x3, blocking collectives, exchange(): return lax.all_to_all(pieces, axis, 0, 0, tiled=True).reshape(x.shape)  50.9 us
    all_to_all x3, starting transfers between devices, exchange(): return lax.all_to_all(pieces, axis, 0, 0, tiled=True).reshape(x.shape)  27.8 us
    pallas_call x17, Pallas kernels, call(): pl.pallas_call(kernel, out_shape=outs, in_specs=specs, out_specs=[pl.Bloc...  27.3 us
    all_to_all x2, blocking collectives, residual_of(): lax.all_to_all(pieces, 'blk', 0, 0, tiled=True, axis_index_groups=columns)  23.1 us
    all_to_all x3, waiting for transfers between devices, exchange(): return lax.all_to_all(pieces, axis, 0, 0, tiled=True).reshape(x.shape)  13.1 us
    all_gather x3, blocking collectives, residual_of(): both = lax.all_gather(stack, 'blk', axis_index_groups=pairs, tiled=True)  12.1 us
    all_to_all x1, starting transfers between devices, residual_of(): lax.all_to_all(pieces, 'blk', 0, 0, tiled=True, axis_index_groups=columns)  10 us
  transfers between devices with their start and end apart: 4, of which 2 were waited for; matrix products, arithmetic and copies ran while one was open for 0% of the time, Pallas kernels for 7%

profile of v4, /device:TPU:1, one launch (start us, length us, event | category | flops | bytes accessed | tf_op | source)
XLA Modules:
  0.0 230.9 jit_solution(226079706039026012)
XLA Ops:
  0.6 0.0 copy-start.6
  0.6 0.7 copy-done.6
  1.3 0.0 copy-start.4
  1.3 1.1 copy-done.4
  2.4 0.0 copy-start.5
  2.4 1.0 copy-done.5
  3.4 4.2 %features.1 = (bf16[512,896]{1,0:T(8,128)(2,1)S(1)}, f32[1280,128]{1,0:T(8,128)}) custom-call(bf16[28,4,1792]{2,1,0:T(4,128)(2,1)S(1)} %bitcast.40, bf16[576,512]{1,0:T(8,128)(2,1)S(1)} %bitcast.39, f32[1,512]{1,0:T(1,128)S(1)} %bitcast.41), custom_call_target="tpu_custom_call" | custom-call | flops 2000000000 | bytes 2566144 | tf_op jit(solution)/shard_map/features/pallas_call | solution.py:60
  7.6 0.0 copy-start
  7.6 10.6 %all-to-all-start.2 = ((f32[32,40,128]{2,1,0:T(8,128)}), f32[32,40,128]{2,1,0:T(8,128)S(1)}, u32[]{:S(2)}, u32[]{:S(2)}) async-start(f32[32,40,128]{2,1,0:T(8,128)} %bitcast.10), calls=%async_computation.2 | async-start | bytes 1310720 | tf_op jit(solution)/shard_map/all_to_all | solution.py:317
  18.2 0.0 copy-done
  18.2 0.4 predict.3
  18.7 2.8 %all_gather.18.both = bf16[2304,128]{1,0:T(8,128)(2,1)S(1)} all-gather(bf16[1152,128]{1,0:T(8,128)(2,1)S(1)} %predict.3), channel_id=1, replica_groups={{0,1},{2,3},{4,5},{6,7},{8,9},{10,11},{12,13},{14,15},{16,17},{18,19},{..., dimensions={0}, use_global_device_ids=true | all-gather | bytes 884736 | tf_op jit(solution)/shard_map/all_gather | solution.py:358
  21.5 0.7 chip.3
  22.2 13.1 %all-to-all-done.2 = f32[32,40,128]{2,1,0:T(8,128)S(1)} async-done(((f32[32,40,128]{2,1,0:T(8,128)}), f32[32,40,128]{2,1,0:T(8,128)S(1)}, u32[]{:S(2)}, u32[]{:S(2)}) %all-to-all-start.2) | async-done | bytes 655392 | tf_op jit(solution)/shard_map/all_to_all | solution.py:317
  35.3 10.0 %all-to-all-start = ((bf16[8,72,128]{2,1,0:T(8,128)(2,1)}), bf16[8,72,128]{2,1,0:T(8,128)(2,1)S(1)}, u32[]{:S(2)}, u32[]{:S(2)}) async-start(bf16[8,72,128]{2,1,0:T(8,128)(2,1)} %bitcast.5), calls=%async_computation | async-start | bytes 294912 | tf_op jit(solution)/shard_map/all_to_all | solution.py:363
  45.3 0.9 gram.1
  46.2 7.2 %all-to-all-done = bf16[8,72,128]{2,1,0:T(8,128)(2,1)S(1)} async-done(((bf16[8,72,128]{2,1,0:T(8,128)(2,1)}), bf16[8,72,128]{2,1,0:T(8,128)(2,1)S(1)}, u32[]{:S(2)}, u32[]{:S(2)}) %all-to-all-start) | async-done | bytes 147488 | tf_op jit(solution)/shard_map/all_to_all | solution.py:363
  53.4 7.7 %all-to-all-start.3 = ((f32[32,40,128]{2,1,0:T(8,128)}), f32[32,40,128]{2,1,0:T(8,128)S(1)}, u32[]{:S(2)}, u32[]{:S(2)}) async-start(f32[32,40,128]{2,1,0:T(8,128)} %bitcast.12), calls=%async_computation.3 | async-start | bytes 1310720 | tf_op jit(solution)/shard_map/all_to_all | solution.py:317
  61.1 0.0 copy-start.7
  61.1 0.7 copy-done.7
  61.8 0.1 residual.3
  61.9 18.2 %all_gather.19.r_0_ = bf16[1152,128]{1,0:T(8,128)(2,1)S(1)} all-gather(bf16[72,128]{1,0:T(8,128)(2,1)S(1)} %residual.3), channel_id=1, replica_groups=mesh['img'=32,'blk'=16] {'blk'}, dimensions={0}, use_global_device_ids=true | all-gather | bytes 313344 | tf_op jit(solution)/shard_map/all_gather | solution.py:368
  80.1 1.2 project.2
  81.4 0.0 all-to-all-done.3
  81.4 0.0 copy-start.2
  81.4 9.5 %all-to-all-start.1 = ((f32[32,24,128]{2,1,0:T(8,128)}), f32[32,24,128]{2,1,0:T(8,128)S(1)}, u32[]{:S(2)}, u32[]{:S(2)}) async-start(f32[32,24,128]{2,1,0:T(8,128)} %bitcast.8), calls=%async_computation.1 | async-start | bytes 786432 | tf_op jit(solution)/shard_map/all_to_all | solution.py:317
  90.9 0.0 copy-done.2
  90.9 0.0 copy-start.3
  90.9 1.1 copy-done.3
  92.0 13.9 %inverse.1 = (bf16[1024,512]{1,0:T(8,128)(2,1)S(1)}, bf16[1024,512]{1,0:T(8,128)(2,1)S(1)}) custom-call(f32[1280,128]{1,0:T(8,128)S(1)} %bitcast.31), custom_call_target="tpu_custom_call" | custom-call | flops 14000000000 | bytes 2752512 | tf_op jit(solution)/shard_map/inverse/pallas_call | solution.py:60
  105.9 0.0 all-to-all-done.1
  105.9 0.0 copy-start.1
  105.9 1.0 copy-done.1
  106.9 1.2 solve.2
  108.1 18.4 %all_to_all.45 = bf16[32,24,128]{2,1,0:T(8,128)(2,1)S(1)} all-to-all(bf16[32,24,128]{2,1,0:T(8,128)(2,1)S(1)} %bitcast.38), channel_id=1, replica_groups=mesh['img'=32,'blk'=16] {'img'}, dimensions={0} | all-to-all | bytes 393216 | tf_op jit(solution)/shard_map/all_to_all | solution.py:317
  126.5 0.5 predict.4
  127.0 4.7 %all_gather.20.both = bf16[2304,128]{1,0:T(8,128)(2,1)S(1)} all-gather(bf16[1152,128]{1,0:T(8,128)(2,1)S(1)} %predict.4), channel_id=1, replica_groups={{0,1},{2,3},{4,5},{6,7},{8,9},{10,11},{12,13},{14,15},{16,17},{18,19},{..., dimensions={0}, use_global_device_ids=true | all-gather | bytes 884736 | tf_op jit(solution)/shard_map/all_gather | solution.py:358
  131.7 11.5 %all_to_all.46 = bf16[8,72,128]{2,1,0:T(8,128)(2,1)S(1)} all-to-all(bf16[8,72,128]{2,1,0:T(8,128)(2,1)S(1)} %bitcast.32), channel_id=1, replica_groups={{0,2,4,6,8,10,12,14},{1,3,5,7,9,11,13,15},{16,18,20,22,24,26,28,30},{17..., dimensions={0} | all-to-all | bytes 294912 | tf_op jit(solution)/shard_map/all_to_all | solution.py:363
  143.3 0.1 residual.4
  143.3 17.4 %all_gather.21.r_0_ = bf16[1152,128]{1,0:T(8,128)(2,1)S(1)} all-gather(bf16[72,128]{1,0:T(8,128)(2,1)S(1)} %residual.4), channel_id=1, replica_groups=mesh['img'=32,'blk'=16] {'blk'}, dimensions={0}, use_global_device_ids=true | all-gather | bytes 313344 | tf_op jit(solution)/shard_map/all_gather | solution.py:368
  160.7 0.5 project.3
  161.2 15.8 %all_to_all.47 = f32[32,24,128]{2,1,0:T(8,128)S(1)} all-to-all(f32[32,24,128]{2,1,0:T(8,128)S(1)} %bitcast.27), channel_id=1, replica_groups=mesh['img'=32,'blk'=16] {'img'}, dimensions={0} | all-to-all | bytes 786432 | tf_op jit(solution)/shard_map/all_to_all | solution.py:317
  177.0 1.8 solve.3
  178.8 16.7 %all_to_all.48 = bf16[32,24,128]{2,1,0:T(8,128)(2,1)S(1)} all-to-all(bf16[32,24,128]{2,1,0:T(8,128)(2,1)S(1)} %bitcast.37), channel_id=1, replica_groups=mesh['img'=32,'blk'=16] {'img'}, dimensions={0} | all-to-all | bytes 393216 | tf_op jit(solution)/shard_map/all_to_all | solution.py:317
  195.4 0.9 predict.5
  196.3 4.6 %all_gather.22.both = bf16[2304,128]{1,0:T(8,128)(2,1)S(1)} all-gather(bf16[1152,128]{1,0:T(8,128)(2,1)S(1)} %get-tuple-element.19), channel_id=1, replica_groups={{0,1},{2,3},{4,5},{6,7},{8,9},{10,11},{12,13},{14,15},{16,17},{18,19},{..., dimensions={0}, use_global_device_ids=true | all-gather | bytes 884736 | tf_op jit(solution)/shard_map/all_gather | solution.py:358
  201.0 11.6 %all_to_all.49 = bf16[8,72,128]{2,1,0:T(8,128)(2,1)S(1)} all-to-all(bf16[8,72,128]{2,1,0:T(8,128)(2,1)S(1)} %bitcast.33), channel_id=1, replica_groups={{0,2,4,6,8,10,12,14},{1,3,5,7,9,11,13,15},{16,18,20,22,24,26,28,30},{17..., dimensions={0} | all-to-all | bytes 294912 | tf_op jit(solution)/shard_map/all_to_all | solution.py:363
  212.6 0.1 residual.5
  212.6 17.4 %all_gather.23.r_0_ = bf16[1152,128]{1,0:T(8,128)(2,1)S(1)} all-gather(bf16[72,128]{1,0:T(8,128)(2,1)S(1)} %residual.5), channel_id=1, replica_groups=mesh['img'=32,'blk'=16] {'blk'}, dimensions={0}, use_global_device_ids=true | all-gather | bytes 313344 | tf_op jit(solution)/shard_map/all_gather | solution.py:368
  230.0 0.9 output.1
  (3 shorter events, 0.1 us)
Async XLA Ops:
  0.6 0.7 copy-start.6
  1.3 1.1 copy-start.4
  2.4 1.0 copy-start.5
  7.6 10.6 %copy-start = (f32[150,512]{1,0:T(8,128)S(1)}, f32[150,512]{1,0:T(8,128)}, u32[]{:S(2)}) copy-start(f32[150,512]{1,0:T(8,128)} %r_2_.1) | copy-start | bytes 921604
  7.6 27.7 %all-to-all-start.2 = ((f32[32,40,128]{2,1,0:T(8,128)}), f32[32,40,128]{2,1,0:T(8,128)S(1)}, u32[]{:S(2)}, u32[]{:S(2)}) async-start(f32[32,40,128]{2,1,0:T(8,128)} %bitcast.10), calls=%async_computation.2 | async-start | bytes 1310720 | tf_op jit(solution)/shard_map/all_to_all | solution.py:317
  35.3 18.2 %all-to-all-start = ((bf16[8,72,128]{2,1,0:T(8,128)(2,1)}), bf16[8,72,128]{2,1,0:T(8,128)(2,1)S(1)}, u32[]{:S(2)}, u32[]{:S(2)}) async-start(bf16[8,72,128]{2,1,0:T(8,128)(2,1)} %bitcast.5), calls=%async_computation | async-start | bytes 294912 | tf_op jit(solution)/shard_map/all_to_all | solution.py:363
  53.4 27.9 %all-to-all-start.3 = ((f32[32,40,128]{2,1,0:T(8,128)}), f32[32,40,128]{2,1,0:T(8,128)S(1)}, u32[]{:S(2)}, u32[]{:S(2)}) async-start(f32[32,40,128]{2,1,0:T(8,128)} %bitcast.12), calls=%async_computation.3 | async-start | bytes 1310720 | tf_op jit(solution)/shard_map/all_to_all | solution.py:317
  61.1 0.7 copy-start.7
  81.4 9.5 %copy-start.2 = (f32[32,40,128]{2,1,0:T(8,128)}, f32[32,40,128]{2,1,0:T(8,128)S(1)}, u32[]{:S(2)}) copy-start(f32[32,40,128]{2,1,0:T(8,128)S(1)} %all-to-all-done.3) | copy-start | bytes 1966084
  81.4 24.5 %all-to-all-start.1 = ((f32[32,24,128]{2,1,0:T(8,128)}), f32[32,24,128]{2,1,0:T(8,128)S(1)}, u32[]{:S(2)}, u32[]{:S(2)}) async-start(f32[32,24,128]{2,1,0:T(8,128)} %bitcast.8), calls=%async_computation.1 | async-start | bytes 786432 | tf_op jit(solution)/shard_map/all_to_all | solution.py:317
  90.9 1.1 copy-start.3
  105.9 1.0 copy-start.1
